TPU v7x, 32 devices: a whole 2x2x4 slice. The times are simulated.
32 devices in a mesh: group: 2 (over core), trow: 2 (over y), tcol: 8 (over z, x).
Axes of the slice: x: 2, y: 2, z: 4, core: 2. Of those that a mesh axis runs over, the one named last changes fastest.
Arguments:
- displacement: float32 [3, 128, 64, 256], P(None, ('group', 'trow'), 'tcol'), may hold values from -6 to 6
- velocity: float32 [3, 128, 64, 256], P(None, ('group', 'trow'), 'tcol'), may hold values from -6 to 6
- stiffness: float32 [128, 64], P(('group', 'trow'), 'tcol'), may hold values from 4 to 12
- wet_position: float32 [3, 8192], P(None, ('group', 'trow', 'tcol')), may hold values from -6 to 6
- wet_normal: float32 [3, 8192], P(None, ('group', 'trow', 'tcol')), may hold values from -6 to 6
- wet_area: float32 [8192], P(('group', 'trow', 'tcol')), may hold values from 0.022097087 to 0.22097087
- wet_map: int32 [8192], P(('group', 'trow', 'tcol')), may hold values from 0 to 255
Outputs:
- displacement_out: float32 [3, 128, 64, 256], P(None, ('group', 'trow'), 'tcol')
- velocity_out: float32 [3, 128, 64, 256], P(None, ('group', 'trow'), 'tcol')
Inputs may be any that keep to these rules, and one draw needn't show every extreme that they name: Each wet point lies on the patch of nodes of the device that holds it: wet_map gives a * 8 + b for the node (a, b) of that patch.
All inputs are finite; a program needn't handle non-finite values.
Results may differ from a plain program's by a relative error of at most 0.0018.
Values may be sent and summed in bfloat16 or wider, within the bound.
A program may use at most 128 MiB of HBM per device.

v0:
```python
import math

import jax
import jax.numpy as jnp
from jax import lax
from jax.sharding import PartitionSpec as P

LOADS = 64
SUBSTEPS = 4
COUPLED = 2
WET_DEV = 256


SPHERE_AREA = 4.0 * math.pi
SMOOTHING = 0.1
TIME_STEP = 0.3
THICKNESS = 0.5
SPLINE_TAPS = (2.0 / 3.0, -1.0 / 12.0, -1.0 / 12.0, -1.0 / 6.0)


def padded_2(array, sides, width):
    for axis, dim in sides:
        count, length = (lax.axis_size(axis), array.shape[dim])
        up = [(i, (i + 1) % count) for i in range(count - 1)]
        down = [(j, i) for i, j in up]
        last = lax.slice_in_dim(array, length - width, length, axis=dim)
        first = lax.slice_in_dim(array, 0, width, axis=dim)
        before = lax.ppermute(last, axis, up)
        after = lax.ppermute(first, axis, down)
        array = jnp.concatenate([before, array, after], axis=dim)
    return array


def spline_apply(padded, height, breadth, margin):
    middle = padded[:, margin : margin + height, margin : margin + breadth]
    summed = 2.0 * SPLINE_TAPS[0] * middle
    for offset in (1, 2, 3):
        along_rows = (
            padded[:, margin + offset : margin + offset + height, margin : margin + breadth]
            + padded[:, margin - offset : margin - offset + height, margin : margin + breadth]
        )
        along_cols = (
            padded[:, margin : margin + height, margin + offset : margin + offset + breadth]
            + padded[:, margin : margin + height, margin - offset : margin - offset + breadth]
        )
        summed = summed + SPLINE_TAPS[offset] * (along_rows + along_cols)
    return summed


def thickness_term(values, stride):
    above_layer = jnp.concatenate([values[..., stride:], values[..., -stride:]], axis=3)
    below_layer = jnp.concatenate([values[..., :stride], values[..., :-stride]], axis=3)
    return 2.0 * values - above_layer - below_layer


def advance(displacement, velocity, stiffness_grid, loading, in_plane):
    acceleration = -(stiffness_grid * in_plane) - THICKNESS * thickness_term(displacement, LOADS)
    outermost = acceleration[..., -LOADS:] + loading
    acceleration = jnp.concatenate([acceleration[..., :-LOADS], outermost], axis=3)
    velocity = velocity + TIME_STEP * acceleration
    displacement = displacement + TIME_STEP * velocity
    return (displacement, velocity)


def kernel_tile(position, normal, area, targets):
    delta_x = targets[0][None, :] - position[0][:, None]
    delta_y = targets[1][None, :] - position[1][:, None]
    delta_z = targets[2][None, :] - position[2][:, None]
    numerator = (
        normal[0][:, None] * delta_x + normal[1][:, None] * delta_y + normal[2][:, None] * delta_z
    )
    squared = delta_x * delta_x + delta_y * delta_y + delta_z * delta_z + SMOOTHING * SMOOTHING
    weighted = area[:, None] * numerator
    return (weighted / (SPHERE_AREA * squared * jnp.sqrt(squared))).astype(jnp.bfloat16)


def normal_speeds(velocity, wet_normal, wet_map):
    outer_layer = velocity[..., -LOADS:]
    flattened = outer_layer.reshape(3, outer_layer.shape[1] * outer_layer.shape[2], LOADS)
    picked = jnp.take(flattened, wet_map, axis=1)
    speeds = (
        wet_normal[0][:, None] * picked[0]
        + wet_normal[1][:, None] * picked[1]
        + wet_normal[2][:, None] * picked[2]
    )
    return speeds.T


def node_loads(pressure, wet_normal, wet_map, height, breadth):
    node_count = height * breadth
    one_hot = (
        lax.broadcasted_iota(jnp.int32, (node_count, wet_map.shape[0]), 0) == wet_map[None, :]
    ).astype(jnp.float32)
    contribution = -(wet_normal[:, None, :] * pressure[None, :, :])
    loading = jnp.einsum("pw,kqw->kpq", one_hot, contribution, precision=lax.Precision.HIGHEST)
    return loading.reshape(3, height, breadth, LOADS)


def pressure_terms(sources, targets, gathered, block_size, block_count):
    position, normal, area = sources

    def accumulate(block_index, summed):
        tile = kernel_tile(
            position,
            normal,
            area,
            lax.dynamic_slice_in_dim(targets, block_index * block_size, block_size, 1),
        )
        partial_value = jnp.dot(gathered, tile, preferred_element_type=jnp.float32)
        return lax.dynamic_update_slice_in_dim(summed, partial_value, block_index * block_size, 1)

    initial = jnp.zeros((gathered.shape[0], block_size * block_count), jnp.float32)
    return lax.fori_loop(0, block_count, accumulate, initial)


def on_device(displacement, velocity, stiffness, wet_position, wet_normal, wet_area, wet_map):
    height = displacement.shape[1]
    breadth = displacement.shape[2]
    targets = lax.all_gather(wet_position, ("group", "trow"), axis=1, tiled=True)
    sources = (
        lax.all_gather(wet_position, "tcol", axis=1, tiled=True),
        lax.all_gather(wet_normal, "tcol", axis=1, tiled=True),
        lax.all_gather(wet_area, "tcol", axis=0, tiled=True),
    )
    target_count = targets.shape[1]
    factor = 2
    block_size = WET_DEV * factor
    block_count = target_count // block_size
    stiffness_grid = stiffness[None, :, :, None]
    for repeat in range(COUPLED):
        speeds = normal_speeds(velocity, wet_normal, wet_map)
        speed_rounded = speeds.astype(jnp.bfloat16)
        gathered = lax.all_gather(speed_rounded, "tcol", axis=1, tiled=True)
        partial_value = pressure_terms(sources, targets, gathered, block_size, block_count)
        received = lax.psum_scatter(
            partial_value, ("group", "trow"), scatter_dimension=1, tiled=True
        )
        pressure = 0.5 * speeds + received
        loading = node_loads(pressure, wet_normal, wet_map, height, breadth)
        for substep in range(SUBSTEPS):
            padded = padded_2(displacement, ((("group", "trow"), 1), ("tcol", 2)), 3)
            in_plane = spline_apply(padded, height, breadth, 3)
            displacement, velocity = advance(
                displacement, velocity, stiffness_grid, loading, in_plane
            )
    return (displacement, velocity)


def solution(mesh):
    placed = (
        P(None, ("group", "trow"), "tcol", None),
        P(None, ("group", "trow"), "tcol", None),
        P(("group", "trow"), "tcol"),
        P(None, ("group", "trow", "tcol")),
        P(None, ("group", "trow", "tcol")),
        P(("group", "trow", "tcol")),
        P(("group", "trow", "tcol")),
    )
    return jax.shard_map(
        on_device,
        mesh=mesh,
        in_specs=placed,
        out_specs=(
            P(None, ("group", "trow"), "tcol", None),
            P(None, ("group", "trow"), "tcol", None),
        ),
        check_vma=False,
    )
```

profile of v0, /device:TPU:20, one launch (start us, length us, event | category | flops | bytes accessed | tf_op | source)
XLA Modules:
  0.0 485.9 jit_solution(4813544611088728946)
XLA Ops:
  16.2 26.4 %all_gather.19 = f32[3,2048]{1,0:T(4,128)S(1)} all-gather(f32[3,256]{1,0:T(4,128)} %param.17), channel_id=1, replica_groups=mesh['group'=2,'trow'=2,'tcol'=8] {'tcol'}, dimensions={1}, use_global_device_ids=true | all-gather | bytes 27648 | tf_op jit(solution)/shard_map/all_gather | solution.py:122
  42.6 30.7 %all_gather.21 = f32[3,2048]{1,0:T(4,128)S(1)} all-gather(f32[3,256]{1,0:T(4,128)} %param.16), channel_id=1, replica_groups=mesh['group'=2,'trow'=2,'tcol'=8] {'tcol'}, dimensions={1}, use_global_device_ids=true | all-gather | bytes 27648 | tf_op jit(solution)/shard_map/all_gather | solution.py:121
  73.3 10.4 %all_gather.20 = f32[3,1024]{1,0:T(4,128)} all-gather(f32[3,256]{1,0:T(4,128)} %param.16), channel_id=1, replica_groups=mesh['group'=2,'trow'=2,'tcol'=8] {'group','trow'}, dimensions={1}, use_global_device_ids=true | all-gather | bytes 15360 | tf_op jit(solution)/shard_map/all_gather | solution.py:119
  87.0 31.2 %all_gather.22 = bf16[64,2048]{0,1:T(8,128)(2,1)S(1)} all-gather(bf16[64,256]{0,1:T(8,128)(2,1)S(1)} %get-tuple-element.319), channel_id=1, replica_groups=mesh['group'=2,'trow'=2,'tcol'=8] {'tcol'}, dimensions={1}, use_global_device_ids=true | all-gather | bytes 294912 | tf_op jit(solution)/shard_map/all_gather | solution.py:133
  118.4 19.7 %all-gather = f32[8,1,256]{2,1,0:T(1,128)S(1)} all-gather(f32[1,1,256]{2,1,0:T(1,128)S(1)} %bitcast.189), channel_id=1, replica_groups=mesh['group'=2,'trow'=2,'tcol'=8] {'tcol'}, dimensions={0}, use_global_device_ids=true | all-gather | bytes 9216 | tf_op jit(solution)/shard_map/all_gather | solution.py:123
  138.2 11.3 %while.26 = (s32[]{:T(128)}, f32[64,1024]{1,0:T(8,128)S(1)}, f32[2048]{0:T(1024)S(1)}, f32[3,2048]{1,0:T(4,128)S(1)}, f32[3,1024]{1,0:T(4,128)}, /*index=5*/f32[...) while((s32[]{:T(128)}, f32[64,1024]{1,0:T(8,128)S(1)}, ...), condition=%wide.region_1.3_spmd, body=%wide.region_0.0_spmd.sunk | while | flops 154140672 | bytes 567507 | solution.py:113
  139.1 4.7 fusion.287
  144.8 4.7 fusion.287
  160.6 8.2 %collective-permute-done.2 = f32[3,38,3,256]{3,2,1,0:T(4,128)S(1)} collective-permute-done((f32[3,38,3,256]{3,2,1,0:T(4,128)}, f32[3,38,3,256]{3,2,1,0:T(4,128)S(1)}, u32[]{:S(2)}, u32[]{:S(2)}) %collective-permute-start.2) | collective-permute-done | bytes 350240 | tf_op jit(solution)/shard_map/ppermute | solution.py:29
  169.5 5.7 %fusion.156 = f32[3,32,8,256]{3,2,1,0:T(8,128)S(1)} fusion(f32[3,38,8,256]{3,2,1,0:T(8,128)} %copy-done.5, f32[3,38,3,256]{3,2,1,0:T(4,128)} %collective-permute-done.3, f32[3,38,3,256]{3,2,1,0:T(4,128)} %copy-done.16, f32[3,35,8,256]{3,2,1,0:T(8,128)} %copy-done.3, f32[3,35,8,256]{3,2,1,0:T(8,128)S(1)} %get-tuple-element.429, ...), kind=kLoop, calls=%fused_computation.249 | loop fusion | flops 6094848 | bytes 9499648 | tf_op jit(solution)/shard_map/sub | solution.py:57
  193.9 15.6 %collective-permute-done.6 = f32[3,38,3,256]{3,2,1,0:T(4,128)S(1)} collective-permute-done((f32[3,38,3,256]{3,2,1,0:T(4,128)S(1)}, f32[3,38,3,256]{3,2,1,0:T(4,128)S(1)}, u32[]{:S(2)}, u32[]{:S(2)}) %collective-permute-start.6) | collective-permute-done | bytes 350240 | tf_op jit(solution)/shard_map/ppermute | solution.py:29
  223.0 5.2 %collective-permute-start.10 = (f32[3,38,3,256]{3,2,1,0:T(4,128)S(1)}, f32[3,38,3,256]{3,2,1,0:T(4,128)S(1)}, u32[]{:S(2)}, u32[]{:S(2)}) collective-permute-start(f32[3,38,3,256]{3,2,1,0:T(4,128)S(1)} %get-tuple-element.367), channel_id=1, source_target_pairs={{1,0},{2,1},{3,2},{4,3},{5,4},{6,5},{7,6},{9,8},{10,9},{11,10},{12... | collective-permute-start | bytes 1050632 | tf_op jit(solution)/shard_map/ppermute | solution.py:29
  230.5 15.9 %collective-permute-done.10 = f32[3,38,3,256]{3,2,1,0:T(4,128)S(1)} collective-permute-done((f32[3,38,3,256]{3,2,1,0:T(4,128)S(1)}, f32[3,38,3,256]{3,2,1,0:T(4,128)S(1)}, u32[]{:S(2)}, u32[]{:S(2)}) %collective-permute-start.10) | collective-permute-done | bytes 350240 | tf_op jit(solution)/shard_map/ppermute | solution.py:29
  259.2 5.6 %collective-permute-start.14 = (f32[3,38,3,256]{3,2,1,0:T(4,128)S(1)}, f32[3,38,3,256]{3,2,1,0:T(4,128)S(1)}, u32[]{:S(2)}, u32[]{:S(2)}) collective-permute-start(f32[3,38,3,256]{3,2,1,0:T(4,128)S(1)} %get-tuple-element.363), channel_id=1, source_target_pairs={{1,0},{2,1},{3,2},{4,3},{5,4},{6,5},{7,6},{9,8},{10,9},{11,10},{12... | collective-permute-start | bytes 1050632 | tf_op jit(solution)/shard_map/ppermute | solution.py:29
  267.1 15.9 %collective-permute-done.14 = f32[3,38,3,256]{3,2,1,0:T(4,128)S(1)} collective-permute-done((f32[3,38,3,256]{3,2,1,0:T(4,128)S(1)}, f32[3,38,3,256]{3,2,1,0:T(4,128)S(1)}, u32[]{:S(2)}, u32[]{:S(2)}) %collective-permute-start.14) | collective-permute-done | bytes 350240 | tf_op jit(solution)/shard_map/ppermute | solution.py:29
  288.5 29.5 %all_gather.23 = bf16[64,2048]{0,1:T(8,128)(2,1)S(1)} all-gather(bf16[64,256]{0,1:T(8,128)(2,1)S(1)} %get-tuple-element.313), channel_id=1, replica_groups=mesh['group'=2,'trow'=2,'tcol'=8] {'tcol'}, dimensions={1}, use_global_device_ids=true | all-gather | bytes 294912 | tf_op jit(solution)/shard_map/all_gather | solution.py:133
  324.2 11.3 %while.27 = (s32[]{:T(128)}, f32[64,1024]{1,0:T(8,128)S(1)}, f32[2048]{0:T(1024)S(1)}, f32[3,2048]{1,0:T(4,128)S(1)}, f32[3,1024]{1,0:T(4,128)}, /*index=5*/f32[...) while((s32[]{:T(128)}, f32[64,1024]{1,0:T(8,128)S(1)}, ...), condition=%wide.region_4.6_spmd, body=%wide.region_3.5_spmd.sunk | while | flops 154140672 | bytes 567507 | solution.py:113
  325.1 4.7 fusion.291
  330.8 4.7 fusion.291
  343.9 11.3 %collective-permute-done.18 = f32[3,38,3,256]{3,2,1,0:T(4,128)} collective-permute-done((f32[3,38,3,256]{3,2,1,0:T(4,128)}, f32[3,38,3,256]{3,2,1,0:T(4,128)}, u32[]{:S(2)}, u32[]{:S(2)}) %collective-permute-start.18) | collective-permute-done | bytes 350240 | tf_op jit(solution)/shard_map/ppermute | solution.py:29
  359.6 7.9 %reduce-scatter.5.cloned.1.call-done = f32[64,256]{0,1:T(8,128)} async-done(((f32[64,1024]{0,1:T(8,128)}), f32[64,256]{0,1:T(8,128)}) %reduce-scatter.5.cloned.1.call-update) | async-done | bytes 65552 | tf_op jit(solution)/shard_map/reduce_scatter | solution.py:135
  385.6 16.4 %collective-permute-done.22 = f32[3,38,3,256]{3,2,1,0:T(4,128)S(1)} collective-permute-done((f32[3,38,3,256]{3,2,1,0:T(4,128)S(1)}, f32[3,38,3,256]{3,2,1,0:T(4,128)S(1)}, u32[]{:S(2)}, u32[]{:S(2)}) %collective-permute-start.22) | collective-permute-done | bytes 350240 | tf_op jit(solution)/shard_map/ppermute | solution.py:29
  422.0 16.8 %collective-permute-done.26 = f32[3,38,3,256]{3,2,1,0:T(4,128)S(1)} collective-permute-done((f32[3,38,3,256]{3,2,1,0:T(4,128)S(1)}, f32[3,38,3,256]{3,2,1,0:T(4,128)S(1)}, u32[]{:S(2)}, u32[]{:S(2)}) %collective-permute-start.26) | collective-permute-done | bytes 350240 | tf_op jit(solution)/shard_map/ppermute | solution.py:29
  458.0 17.1 %collective-permute-done.30 = f32[3,38,3,256]{3,2,1,0:T(4,128)S(1)} collective-permute-done((f32[3,38,3,256]{3,2,1,0:T(4,128)S(1)}, f32[3,38,3,256]{3,2,1,0:T(4,128)S(1)}, u32[]{:S(2)}, u32[]{:S(2)}) %collective-permute-start.30) | collective-permute-done | bytes 350240 | tf_op jit(solution)/shard_map/ppermute | solution.py:29
  (237 shorter events, 162.2 us)
Async XLA Ops:
  7.2 168.1 %reduce-scatter.3.cloned.1.call-start = ((), (), s32[]{:S(2)}) async-start(), calls=%async_computation.2 | async-start | bytes 655360 | tf_op jit(solution)/shard_map/reduce_scatter | solution.py:135
  8.1 142.5 %collective-permute-start.1 = (f32[3,3,8,256]{3,2,1,0:T(8,128)S(1)}, f32[3,3,8,256]{3,2,1,0:T(8,128)S(1)}, u32[]{:S(2)}, u32[]{:S(2)}) collective-permute-start(f32[3,3,8,256]{3,2,1,0:T(8,128)S(1)} %get-tuple-element.425), channel_id=1, source_target_pairs={{0,8},{8,16},{16,24},{1,9},{9,17},{17,25},{2,10},{10,18},{18,26},{... | collective-permute-start | bytes 221192 | tf_op jit(solution)/shard_map/ppermute | solution.py:28
  10.1 140.9 %collective-permute-start = (f32[3,3,8,256]{3,2,1,0:T(8,128)S(1)}, f32[3,3,8,256]{3,2,1,0:T(8,128)S(1)}, u32[]{:S(2)}, u32[]{:S(2)}) collective-permute-start(f32[3,3,8,256]{3,2,1,0:T(8,128)S(1)} %get-tuple-element.424), channel_id=1, source_target_pairs={{8,0},{16,8},{24,16},{9,1},{17,9},{25,17},{10,2},{18,10},{26,18},{... | collective-permute-start | bytes 221192 | tf_op jit(solution)/shard_map/ppermute | solution.py:29
  150.6 216.9 %reduce-scatter.5.cloned.1.call-start = ((), (), s32[]{:S(2)}) async-start(), calls=%async_computation.3 | async-start | bytes 655360 | tf_op jit(solution)/shard_map/reduce_scatter | solution.py:135
  153.1 15.7 %collective-permute-start.2 = (f32[3,38,3,256]{3,2,1,0:T(4,128)}, f32[3,38,3,256]{3,2,1,0:T(4,128)S(1)}, u32[]{:S(2)}, u32[]{:S(2)}) collective-permute-start(f32[3,38,3,256]{3,2,1,0:T(4,128)} %get-tuple-element.373), channel_id=1, source_target_pairs={{1,0},{2,1},{3,2},{4,3},{5,4},{6,5},{7,6},{9,8},{10,9},{11,10},{12... | collective-permute-start | bytes 1050632 | tf_op jit(solution)/shard_map/ppermute | solution.py:29
  155.4 13.4 %collective-permute-start.3 = (f32[3,38,3,256]{3,2,1,0:T(4,128)}, f32[3,38,3,256]{3,2,1,0:T(4,128)}, u32[]{:S(2)}, u32[]{:S(2)}) collective-permute-start(f32[3,38,3,256]{3,2,1,0:T(4,128)} %get-tuple-element.374), channel_id=1, source_target_pairs={{0,1},{1,2},{2,3},{3,4},{4,5},{5,6},{6,7},{8,9},{9,10},{10,11},{11... | collective-permute-start | bytes 1050632 | tf_op jit(solution)/shard_map/ppermute | solution.py:28
  187.1 22.4 %collective-permute-start.6 = (f32[3,38,3,256]{3,2,1,0:T(4,128)S(1)}, f32[3,38,3,256]{3,2,1,0:T(4,128)S(1)}, u32[]{:S(2)}, u32[]{:S(2)}) collective-permute-start(f32[3,38,3,256]{3,2,1,0:T(4,128)S(1)} %get-tuple-element.371), channel_id=1, source_target_pairs={{1,0},{2,1},{3,2},{4,3},{5,4},{6,5},{7,6},{9,8},{10,9},{11,10},{12... | collective-permute-start | bytes 1050632 | tf_op jit(solution)/shard_map/ppermute | solution.py:29
  191.4 18.1 %collective-permute-start.7 = (f32[3,38,3,256]{3,2,1,0:T(4,128)S(1)}, f32[3,38,3,256]{3,2,1,0:T(4,128)S(1)}, u32[]{:S(2)}, u32[]{:S(2)}) collective-permute-start(f32[3,38,3,256]{3,2,1,0:T(4,128)S(1)} %get-tuple-element.372), channel_id=1, source_target_pairs={{0,1},{1,2},{2,3},{3,4},{4,5},{5,6},{6,7},{8,9},{9,10},{10,11},{11... | collective-permute-start | bytes 1050632 | tf_op jit(solution)/shard_map/ppermute | solution.py:28
  223.0 23.5 %collective-permute-start.10 = (f32[3,38,3,256]{3,2,1,0:T(4,128)S(1)}, f32[3,38,3,256]{3,2,1,0:T(4,128)S(1)}, u32[]{:S(2)}, u32[]{:S(2)}) collective-permute-start(f32[3,38,3,256]{3,2,1,0:T(4,128)S(1)} %get-tuple-element.367), channel_id=1, source_target_pairs={{1,0},{2,1},{3,2},{4,3},{5,4},{6,5},{7,6},{9,8},{10,9},{11,10},{12... | collective-permute-start | bytes 1050632 | tf_op jit(solution)/shard_map/ppermute | solution.py:29
  228.1 18.5 %collective-permute-start.11 = (f32[3,38,3,256]{3,2,1,0:T(4,128)S(1)}, f32[3,38,3,256]{3,2,1,0:T(4,128)S(1)}, u32[]{:S(2)}, u32[]{:S(2)}) collective-permute-start(f32[3,38,3,256]{3,2,1,0:T(4,128)S(1)} %get-tuple-element.368), channel_id=1, source_target_pairs={{0,1},{1,2},{2,3},{3,4},{4,5},{5,6},{6,7},{8,9},{9,10},{10,11},{11... | collective-permute-start | bytes 1050632 | tf_op jit(solution)/shard_map/ppermute | solution.py:28
  259.2 23.8 %collective-permute-start.14 = (f32[3,38,3,256]{3,2,1,0:T(4,128)S(1)}, f32[3,38,3,256]{3,2,1,0:T(4,128)S(1)}, u32[]{:S(2)}, u32[]{:S(2)}) collective-permute-start(f32[3,38,3,256]{3,2,1,0:T(4,128)S(1)} %get-tuple-element.363), channel_id=1, source_target_pairs={{1,0},{2,1},{3,2},{4,3},{5,4},{6,5},{7,6},{9,8},{10,9},{11,10},{12... | collective-permute-start | bytes 1050632 | tf_op jit(solution)/shard_map/ppermute | solution.py:29
  264.7 18.4 %collective-permute-start.15 = (f32[3,38,3,256]{3,2,1,0:T(4,128)S(1)}, f32[3,38,3,256]{3,2,1,0:T(4,128)S(1)}, u32[]{:S(2)}, u32[]{:S(2)}) collective-permute-start(f32[3,38,3,256]{3,2,1,0:T(4,128)S(1)} %get-tuple-element.364), channel_id=1, source_target_pairs={{0,1},{1,2},{2,3},{3,4},{4,5},{5,6},{6,7},{8,9},{9,10},{10,11},{11... | collective-permute-start | bytes 1050632 | tf_op jit(solution)/shard_map/ppermute | solution.py:28
  318.2 17.3 %collective-permute-start.16 = (f32[3,3,8,256]{3,2,1,0:T(8,128)S(1)}, f32[3,3,8,256]{3,2,1,0:T(8,128)S(1)}, u32[]{:S(2)}, u32[]{:S(2)}) collective-permute-start(f32[3,3,8,256]{3,2,1,0:T(8,128)S(1)} %get-tuple-element.397), channel_id=1, source_target_pairs={{8,0},{16,8},{24,16},{9,1},{17,9},{25,17},{10,2},{18,10},{26,18},{... | collective-permute-start | bytes 221192 | tf_op jit(solution)/shard_map/ppermute | solution.py:29
  322.0 13.5 %collective-permute-start.17 = (f32[3,3,8,256]{3,2,1,0:T(8,128)S(1)}, f32[3,3,8,256]{3,2,1,0:T(8,128)S(1)}, u32[]{:S(2)}, u32[]{:S(2)}) collective-permute-start(f32[3,3,8,256]{3,2,1,0:T(8,128)S(1)} %get-tuple-element.398), channel_id=1, source_target_pairs={{0,8},{8,16},{16,24},{1,9},{9,17},{17,25},{2,10},{10,18},{18,26},{... | collective-permute-start | bytes 221192 | tf_op jit(solution)/shard_map/ppermute | solution.py:28
  336.5 18.7 %collective-permute-start.18 = (f32[3,38,3,256]{3,2,1,0:T(4,128)}, f32[3,38,3,256]{3,2,1,0:T(4,128)}, u32[]{:S(2)}, u32[]{:S(2)}) collective-permute-start(f32[3,38,3,256]{3,2,1,0:T(4,128)} %get-tuple-element.359), channel_id=1, source_target_pairs={{1,0},{2,1},{3,2},{4,3},{5,4},{6,5},{7,6},{9,8},{10,9},{11,10},{12... | collective-permute-start | bytes 1050632 | tf_op jit(solution)/shard_map/ppermute | solution.py:29
  339.7 15.5 %collective-permute-start.19 = (f32[3,38,3,256]{3,2,1,0:T(4,128)S(1)}, f32[3,38,3,256]{3,2,1,0:T(4,128)}, u32[]{:S(2)}, u32[]{:S(2)}) collective-permute-start(f32[3,38,3,256]{3,2,1,0:T(4,128)S(1)} %get-tuple-element.360), channel_id=1, source_target_pairs={{0,1},{1,2},{2,3},{3,4},{4,5},{5,6},{6,7},{8,9},{9,10},{10,11},{11... | collective-permute-start | bytes 1050632 | tf_op jit(solution)/shard_map/ppermute | solution.py:28
  372.8 6.2 %collective-permute-start.21 = (f32[3,3,8,256]{3,2,1,0:T(8,128)S(1)}, f32[3,3,8,256]{3,2,1,0:T(8,128)S(1)}, u32[]{:S(2)}, u32[]{:S(2)}) collective-permute-start(f32[3,3,8,256]{3,2,1,0:T(8,128)S(1)} %get-tuple-element.392), channel_id=1, source_target_pairs={{0,8},{8,16},{16,24},{1,9},{9,17},{17,25},{2,10},{10,18},{18,26},{... | collective-permute-start | bytes 221192 | tf_op jit(solution)/shard_map/ppermute | solution.py:28
  379.3 22.7 %collective-permute-start.22 = (f32[3,38,3,256]{3,2,1,0:T(4,128)S(1)}, f32[3,38,3,256]{3,2,1,0:T(4,128)S(1)}, u32[]{:S(2)}, u32[]{:S(2)}) collective-permute-start(f32[3,38,3,256]{3,2,1,0:T(4,128)S(1)} %get-tuple-element.355), channel_id=1, source_target_pairs={{1,0},{2,1},{3,2},{4,3},{5,4},{6,5},{7,6},{9,8},{10,9},{11,10},{12... | collective-permute-start | bytes 1050632 | tf_op jit(solution)/shard_map/ppermute | solution.py:29
  382.7 19.4 %collective-permute-start.23 = (f32[3,38,3,256]{3,2,1,0:T(4,128)S(1)}, f32[3,38,3,256]{3,2,1,0:T(4,128)S(1)}, u32[]{:S(2)}, u32[]{:S(2)}) collective-permute-start(f32[3,38,3,256]{3,2,1,0:T(4,128)S(1)} %get-tuple-element.356), channel_id=1, source_target_pairs={{0,1},{1,2},{2,3},{3,4},{4,5},{5,6},{6,7},{8,9},{9,10},{10,11},{11... | collective-permute-start | bytes 1050632 | tf_op jit(solution)/shard_map/ppermute | solution.py:28
  415.0 23.8 %collective-permute-start.26 = (f32[3,38,3,256]{3,2,1,0:T(4,128)S(1)}, f32[3,38,3,256]{3,2,1,0:T(4,128)S(1)}, u32[]{:S(2)}, u32[]{:S(2)}) collective-permute-start(f32[3,38,3,256]{3,2,1,0:T(4,128)S(1)} %get-tuple-element.351), channel_id=1, source_target_pairs={{1,0},{2,1},{3,2},{4,3},{5,4},{6,5},{7,6},{9,8},{10,9},{11,10},{12... | collective-permute-start | bytes 1050632 | tf_op jit(solution)/shard_map/ppermute | solution.py:29
  419.3 19.7 %collective-permute-start.27 = (f32[3,38,3,256]{3,2,1,0:T(4,128)S(1)}, f32[3,38,3,256]{3,2,1,0:T(4,128)S(1)}, u32[]{:S(2)}, u32[]{:S(2)}) collective-permute-start(f32[3,38,3,256]{3,2,1,0:T(4,128)S(1)} %get-tuple-element.352), channel_id=1, source_target_pairs={{0,1},{1,2},{2,3},{3,4},{4,5},{5,6},{6,7},{8,9},{9,10},{10,11},{11... | collective-permute-start | bytes 1050632 | tf_op jit(solution)/shard_map/ppermute | solution.py:28
  444.7 6.2 %collective-permute-start.29 = (f32[3,3,8,256]{3,2,1,0:T(8,128)S(1)}, f32[3,3,8,256]{3,2,1,0:T(8,128)S(1)}, u32[]{:S(2)}, u32[]{:S(2)}) collective-permute-start(f32[3,3,8,256]{3,2,1,0:T(8,128)S(1)} %get-tuple-element.380), channel_id=1, source_target_pairs={{0,8},{8,16},{16,24},{1,9},{9,17},{17,25},{2,10},{10,18},{18,26},{... | collective-permute-start | bytes 221192 | tf_op jit(solution)/shard_map/ppermute | solution.py:28
  451.2 23.8 %collective-permute-start.30 = (f32[3,38,3,256]{3,2,1,0:T(4,128)S(1)}, f32[3,38,3,256]{3,2,1,0:T(4,128)S(1)}, u32[]{:S(2)}, u32[]{:S(2)}) collective-permute-start(f32[3,38,3,256]{3,2,1,0:T(4,128)S(1)} %get-tuple-element.347), channel_id=1, source_target_pairs={{1,0},{2,1},{3,2},{4,3},{5,4},{6,5},{7,6},{9,8},{10,9},{11,10},{12... | collective-permute-start | bytes 1050632 | tf_op jit(solution)/shard_map/ppermute | solution.py:29
  455.5 19.7 %collective-permute-start.31 = (f32[3,38,3,256]{3,2,1,0:T(4,128)S(1)}, f32[3,38,3,256]{3,2,1,0:T(4,128)S(1)}, u32[]{:S(2)}, u32[]{:S(2)}) collective-permute-start(f32[3,38,3,256]{3,2,1,0:T(4,128)S(1)} %get-tuple-element.348), channel_id=1, source_target_pairs={{0,1},{1,2},{2,3},{3,4},{4,5},{5,6},{6,7},{8,9},{9,10},{10,11},{11... | collective-permute-start | bytes 1050632 | tf_op jit(solution)/shard_map/ppermute | solution.py:28
  (44 other events, 660.3 us)
Sparse Core Ops, SparseCore 0:
  150.7 23.3 reduce-scatter.2
  343.8 23.6 reduce-scatter.4
where the time goes:
time: 491 us; the launch traced here: 486 us
  waiting for transfers between devices  150 us (31%)
  blocking collectives  148 us (30%)
  starting transfers between devices  97.2 us (20%)
  other arithmetic  33 us (7%)
  local copies, waits for them, and re-layouts  22.9 us (5%)
  matrix products  19.5 us (4%)
  between operations  15.3 us (3%)
    ppermute x16, waiting for transfers between devices, padded_2(): after = lax.ppermute(first, axis, down)  118 us
    ppermute x16, starting transfers between devices, padded_2(): after = lax.ppermute(first, axis, down)  60.9 us
    all_gather x2, blocking collectives, on_device(): gathered = lax.all_gather(speed_rounded, 'tcol', axis=1, tiled=True)  60.8 us
    ppermute x16, starting transfers between devices, padded_2(): before = lax.ppermute(last, axis, up)  36.2 us
    all_gather x1, blocking collectives, on_device(): lax.all_gather(wet_position, 'tcol', axis=1, tiled=True)  30.7 us
    all_gather x1, blocking collectives, on_device(): lax.all_gather(wet_normal, 'tcol', axis=1, tiled=True)  26.4 us
    ppermute x16, waiting for transfers between devices, padded_2(): before = lax.ppermute(last, axis, up)  24.4 us
    all_gather x1, blocking collectives, on_device(): lax.all_gather(wet_area, 'tcol', axis=0, tiled=True)  19.7 us
  transfers between devices with their start and end apart: 34, of which 23 were waited for; matrix products, arithmetic and copies ran while one was open for 10% of the time, Pallas kernels for 0%

commit v1 on v0

v1 whole, which is shorter than its diff:
```python
import functools
import math

import jax
import jax.numpy as jnp
from jax import lax
from jax.experimental import pallas as pl
from jax.experimental.pallas import tpu as pltpu
from jax.sharding import PartitionSpec as P

LOADS = 64
SUBSTEPS = 4
COUPLED = 2

SPHERE_AREA = 4.0 * math.pi
SMOOTHING = 0.1
TIME_STEP = 0.3
THICKNESS = 0.5
SPLINE_TAPS = (2.0 / 3.0, -1.0 / 12.0, -1.0 / 12.0, -1.0 / 6.0)
REACH = 3
PAD = 8
MESH = pl.DeviceIdType.MESH
VMEM = pltpu.VMEM


def row_device(index, trow_count):
    return {"group": index // trow_count, "trow": lax.rem(index, trow_count)}


def whole_spec():
    return pl.BlockSpec(memory_space=pltpu.VMEM)


def gather_kernel(shape, with_geometry, *refs):
    col_count, row_count, trow_count = shape
    if with_geometry:
        (geometry, speeds, all_speeds, sources, targets, send, recv) = refs
        col_pairs = ((speeds, all_speeds), (geometry, sources))
    else:
        (speeds, all_speeds, send, recv) = refs
        col_pairs = ((speeds, all_speeds),)
    col = lax.axis_index("tcol")
    row = lax.axis_index("group") * trow_count + lax.axis_index("trow")
    barrier = pltpu.get_barrier_semaphore()

    @pl.loop(1, col_count)
    def _(d):
        pl.semaphore_signal(
            barrier, inc=1, device_id={"tcol": lax.rem(col + d, col_count)}, device_id_type=MESH
        )

    peers = col_count - 1
    if with_geometry:

        @pl.loop(1, row_count)
        def _(d):
            peer = lax.rem(row + d, row_count)
            pl.semaphore_signal(
                barrier, inc=1, device_id=row_device(peer, trow_count), device_id_type=MESH
            )

        peers = peers + row_count - 1
    pl.semaphore_wait(barrier, peers)

    def col_copy(which, d):
        source, destination = col_pairs[which]
        return pltpu.make_async_remote_copy(
            src_ref=source,
            dst_ref=destination.at[col],
            send_sem=send.at[which, d],
            recv_sem=recv.at[which, d],
            device_id={"tcol": lax.rem(col + d, col_count)},
            device_id_type=MESH,
        )

    def row_copy(d):
        return pltpu.make_async_remote_copy(
            src_ref=geometry,
            dst_ref=targets.at[row],
            send_sem=send.at[2, d],
            recv_sem=recv.at[2, d],
            device_id=row_device(lax.rem(row + d, row_count), trow_count),
            device_id_type=MESH,
        )

    if with_geometry:

        @pl.loop(1, row_count)
        def _(d):
            row_copy(d).start()

    for which in reversed(range(len(col_pairs))):

        @pl.loop(1, col_count)
        def _(d):
            col_copy(which, d).start()

        source, destination = col_pairs[which]
        destination[col] = source[...]
    if with_geometry:
        targets[row] = geometry[...]

        @pl.loop(1, row_count)
        def _(d):
            row_copy(d).wait()

    for which in range(len(col_pairs)):

        @pl.loop(1, col_count)
        def _(d):
            col_copy(which, d).wait()


def gather(shape, geometry, speeds, collective_id):
    col_count, row_count, _ = shape
    with_geometry = geometry is not None
    out_shape = [jax.ShapeDtypeStruct((col_count,) + speeds.shape, speeds.dtype)]
    if with_geometry:
        out_shape.append(jax.ShapeDtypeStruct((col_count,) + geometry.shape, geometry.dtype))
        out_shape.append(jax.ShapeDtypeStruct((row_count,) + geometry.shape, geometry.dtype))
    operands = (geometry, speeds) if with_geometry else (speeds,)
    slots = max(col_count, row_count)
    return pl.pallas_call(
        functools.partial(gather_kernel, shape, with_geometry),
        out_shape=out_shape,
        in_specs=[whole_spec()] * len(operands),
        out_specs=[whole_spec()] * len(out_shape),
        scratch_shapes=[
            pltpu.SemaphoreType.DMA((3, slots)),
            pltpu.SemaphoreType.DMA((3, slots)),
        ],
        compiler_params=pltpu.CompilerParams(
            collective_id=collective_id, has_side_effects=True
        ),
        name="gather_geometry" if with_geometry else "gather_speeds",
    )(*operands)


def tile_kernel(source_ref, target_ref, speeds_ref, tile_ref, partial_ref):
    count, _, size = speeds_ref.shape
    tx = target_ref[0, 0:1, :]
    ty = target_ref[0, 1:2, :]
    tz = target_ref[0, 2:3, :]
    partial_ref[...] = jnp.zeros_like(partial_ref)
    chunk = 64

    @pl.loop(0, count)
    def _(block):
        @pl.loop(0, size // chunk)
        def _(part):
            start = pl.multiple_of(block * size + part * chunk, chunk)
            rows = pl.ds(start, chunk)
            dx = tx - source_ref[rows, 0:1]
            dy = ty - source_ref[rows, 1:2]
            dz = tz - source_ref[rows, 2:3]
            numerator = (
                source_ref[rows, 3:4] * dx + source_ref[rows, 4:5] * dy + source_ref[rows, 5:6] * dz
            )
            squared = dx * dx + dy * dy + dz * dz + SMOOTHING * SMOOTHING
            inverse = lax.rsqrt(squared)
            value = numerator * inverse * (inverse * inverse)
            tile_ref[0, rows, :] = value.astype(jnp.bfloat16)

        rows = pl.ds(pl.multiple_of(block * size, size), size)
        partial_ref[0] += jnp.dot(
            speeds_ref[block], tile_ref[0, rows, :], preferred_element_type=jnp.float32
        )


def product_kernel(speeds_ref, tile_ref, partial_ref):
    count, _, size = speeds_ref.shape
    partial_ref[...] = jnp.zeros_like(partial_ref)

    @pl.loop(0, count)
    def _(block):
        rows = pl.ds(pl.multiple_of(block * size, size), size)
        partial_ref[0] += jnp.dot(
            speeds_ref[block], tile_ref[0, rows, :], preferred_element_type=jnp.float32
        )


def fixed(shape):
    return pl.BlockSpec(shape, lambda r: (0,) * len(shape))


def sliced(shape):
    return pl.BlockSpec((1,) + shape[1:], lambda r: (r, 0, 0))


def tile_and_product(sources, targets, speeds):
    row_count, _, size = targets.shape
    loads = speeds.shape[1]
    tile_shape = (row_count, sources.shape[0], size)
    partial_shape = (row_count, loads, size)
    return pl.pallas_call(
        tile_kernel,
        grid=(row_count,),
        out_shape=(
            jax.ShapeDtypeStruct(tile_shape, jnp.bfloat16),
            jax.ShapeDtypeStruct(partial_shape, jnp.float32),
        ),
        in_specs=[fixed(sources.shape), sliced(targets.shape), fixed(speeds.shape)],
        out_specs=(sliced(tile_shape), sliced(partial_shape)),
        name="tile_and_product",
    )(sources, targets, speeds)


def product(tiles, speeds):
    row_count, _, size = tiles.shape
    partial_shape = (row_count, speeds.shape[1], size)
    return pl.pallas_call(
        product_kernel,
        grid=(row_count,),
        out_shape=jax.ShapeDtypeStruct(partial_shape, jnp.float32),
        in_specs=[fixed(speeds.shape), sliced(tiles.shape)],
        out_specs=sliced(partial_shape),
        name="product",
    )(speeds, tiles)


def reduce_kernel(shape, partial_ref, out_ref, held, send, recv):
    _, row_count, trow_count = shape
    row = lax.axis_index("group") * trow_count + lax.axis_index("trow")
    barrier = pltpu.get_barrier_semaphore()

    @pl.loop(1, row_count)
    def _(d):
        peer = lax.rem(row + d, row_count)
        pl.semaphore_signal(
            barrier, inc=1, device_id=row_device(peer, trow_count), device_id_type=MESH
        )

    pl.semaphore_wait(barrier, row_count - 1)

    def copy(d):
        peer = lax.rem(row + d, row_count)
        return pltpu.make_async_remote_copy(
            src_ref=partial_ref.at[peer],
            dst_ref=held.at[d],
            send_sem=send.at[d],
            recv_sem=recv.at[d],
            device_id=row_device(peer, trow_count),
            device_id_type=MESH,
        )

    @pl.loop(1, row_count)
    def _(d):
        copy(d).start()

    out_ref[...] = partial_ref[row]

    @pl.loop(1, row_count)
    def _(d):
        copy(d).wait()
        out_ref[...] += held[d]


def reduce_scatter(shape, partial_value, collective_id):
    row_count = shape[1]
    block = partial_value.shape[1:]
    return pl.pallas_call(
        functools.partial(reduce_kernel, shape),
        out_shape=jax.ShapeDtypeStruct(block, jnp.float32),
        in_specs=[whole_spec()],
        out_specs=whole_spec(),
        scratch_shapes=[
            VMEM((row_count,) + block, jnp.float32),
            pltpu.SemaphoreType.DMA((row_count,)),
            pltpu.SemaphoreType.DMA((row_count,)),
        ],
        compiler_params=pltpu.CompilerParams(
            collective_id=collective_id, has_side_effects=True
        ),
        name="reduce_scatter",
    )(partial_value)


def substeps_kernel(
    shape, u_in, v_in, stiff_ref, load_ref, u_out, v_out, field, work,
    col_out, col_in, row_out, row_in, send, recv
):
    col_count, row_count, trow_count = shape
    parts, breadth, height, width = u_in.shape
    half = width // 2
    col = lax.axis_index("tcol")
    row = lax.axis_index("group") * trow_count + lax.axis_index("trow")
    present = (col > 0, col < col_count - 1, row > 0, row < row_count - 1)
    peers = (
        {"tcol": jnp.maximum(col - 1, 0)},
        {"tcol": jnp.minimum(col + 1, col_count - 1)},
        row_device(jnp.maximum(row - 1, 0), trow_count),
        row_device(jnp.minimum(row + 1, row_count - 1), trow_count),
    )
    barrier = pltpu.get_barrier_semaphore()
    for side in range(4):

        @pl.when(present[side])
        def _():
            pl.semaphore_signal(barrier, inc=1, device_id=peers[side], device_id_type=MESH)

    field[...] = jnp.zeros_like(field)
    middle = pl.ds(PAD, height)
    for part in range(parts):
        field[part, REACH : REACH + breadth, middle, :] = u_in[part]
    v_out[...] = v_in[...]
    for side in range(2):

        @pl.when(jnp.logical_not(present[side]))
        def _():
            col_in[:, side] = jnp.zeros(
                (col_in.shape[0],) + col_in.shape[2:], col_in.dtype
            )

    pl.semaphore_wait(barrier, sum(here.astype(jnp.int32) for here in present))

    def copy(step, side):
        out_buffer, in_buffer = (col_out, col_in) if side < 2 else (row_out, row_in)
        own, other = side % 2, 1 - side % 2
        return pltpu.make_async_remote_copy(
            src_ref=out_buffer.at[step, own],
            dst_ref=in_buffer.at[step, other],
            send_sem=send.at[step, side],
            recv_sem=recv.at[step, (side // 2) * 2 + other],
            device_id=peers[side],
            device_id_type=MESH,
        )

    def arrival(step, side):
        out_buffer, in_buffer = (col_out, col_in) if side < 2 else (row_out, row_in)
        return pltpu.make_async_remote_copy(
            src_ref=out_buffer.at[step, side % 2],
            dst_ref=in_buffer.at[step, side % 2],
            send_sem=send.at[step, side],
            recv_sem=recv.at[step, side],
            device_id=peers[side],
            device_id_type=MESH,
        )

    lane = lax.broadcasted_iota(jnp.int32, (height, half), 1)
    low = lane < half // 2

    @pl.loop(0, SUBSTEPS)
    def _(step):
        for side, first in ((0, REACH), (1, breadth)):

            @pl.when(present[side])
            def _():
                for part in range(parts):
                    for j in range(REACH):
                        col_out[step, side, part, j] = field[part, first + j, middle, :].astype(
                            col_out.dtype
                        )
                copy(step, side).start()

        for side, first in ((2, PAD), (3, PAD + height - REACH)):

            @pl.when(present[side])
            def _():
                for part in range(parts):
                    for j in range(breadth):
                        row_out[
                            step, side - 2, part, j // 2, (j % 2) * 4 : (j % 2) * 4 + REACH, :
                        ] = field[part, REACH + j, first : first + REACH, :]
                copy(step, side).start()

        def local(index, carry):
            part = index // breadth
            column = lax.rem(index, breadth)
            a = field[part, REACH + column, middle, 0:half]
            b = field[part, REACH + column, middle, half:width]
            turned_a = pltpu.roll(a, half // 2, 1)
            turned_b = pltpu.roll(b, half // 2, 1)
            between = jnp.where(low, turned_a, turned_b)
            edge_a = jnp.where(low, a, turned_a)
            edge_b = jnp.where(low, turned_b, b)
            stiff = stiff_ref[column]
            for lanes, here, edge in ((0, a, edge_a), (1, b, edge_b)):
                cut = pl.ds(lanes * half, half)
                summed = (2.0 * SPLINE_TAPS[0]) * here
                for offset in range(1, REACH + 1):
                    summed = summed + SPLINE_TAPS[offset] * (
                        field[part, REACH + column + offset, middle, cut]
                        + field[part, REACH + column - offset, middle, cut]
                    )
                value = -(stiff * summed) - THICKNESS * (2.0 * here - between - edge)
                if lanes == 1:
                    value = value + load_ref[part, column]
                work[part, column, :, cut] = v_out[part, column, :, cut] + TIME_STEP * value
            return carry

        lax.fori_loop(0, parts * breadth, local, 0)

        for side, first in ((2, PAD - REACH), (3, PAD + height)):

            @pl.when(present[side])
            def _():
                arrival(step, side).wait_recv()
                for part in range(parts):
                    for j in range(breadth):
                        field[part, REACH + j, first : first + REACH, :] = row_in[
                            step, side - 2, part, j // 2, (j % 2) * 4 : (j % 2) * 4 + REACH, :
                        ]

        def along_rows(index, carry):
            part = index // breadth
            column = lax.rem(index, breadth)
            stiff = stiff_ref[column] * (-TIME_STEP)
            for lanes in range(2):
                cut = pl.ds(lanes * half, half)
                summed = 0.0
                for offset in range(1, REACH + 1):
                    summed = summed + SPLINE_TAPS[offset] * (
                        field[part, REACH + column, pl.ds(PAD + offset, height), cut]
                        + field[part, REACH + column, pl.ds(PAD - offset, height), cut]
                    )
                work[part, column, :, cut] += stiff * summed
            return carry

        lax.fori_loop(0, parts * breadth, along_rows, 0)

        for side in range(2):

            @pl.when(present[side])
            def _():
                arrival(step, side).wait_recv()

        def finish(part, carry):
            for column in range(breadth):
                stiff = stiff_ref[column] * (-TIME_STEP)
                for lanes in range(2):
                    cut = pl.ds(lanes * half, half)
                    value = work[part, column, :, cut]
                    summed = None
                    for offset in range(1, REACH + 1):
                        for side, j in ((0, column - offset + REACH), (1, column + offset - breadth)):
                            inside = (column - offset < 0) if side == 0 else (column + offset >= breadth)
                            if inside:
                                term = SPLINE_TAPS[offset] * col_in[
                                    step, side, part, j, :, cut
                                ].astype(jnp.float32)
                                summed = term if summed is None else summed + term
                    if summed is not None:
                        value = value + stiff * summed
                    v_out[part, column, :, cut] = value
                    field[part, REACH + column, middle, cut] += TIME_STEP * value
            return carry

        lax.fori_loop(0, parts, finish, 0)

    for part in range(parts):
        u_out[part] = field[part, REACH : REACH + breadth, middle, :]

    @pl.loop(0, SUBSTEPS)
    def _(step):
        for side in range(4):

            @pl.when(present[side])
            def _():
                copy(step, side).wait_send()


def substeps(shape, displacement, velocity, stiff, loading, collective_id):
    parts, breadth, height, width = displacement.shape
    state = jax.ShapeDtypeStruct(displacement.shape, jnp.float32)
    cols = (SUBSTEPS, 2, parts, REACH, height, width)
    rows = (SUBSTEPS, 2, parts, breadth // 2, 8, width)
    return pl.pallas_call(
        functools.partial(substeps_kernel, shape),
        out_shape=(state, state),
        in_specs=[whole_spec()] * 4,
        out_specs=(whole_spec(), whole_spec()),
        scratch_shapes=[
            VMEM((parts, breadth + 2 * REACH, height + 2 * PAD, width), jnp.float32),
            VMEM((parts, breadth, height, width), jnp.float32),
            VMEM(cols, jnp.bfloat16),
            VMEM(cols, jnp.bfloat16),
            VMEM(rows, jnp.float32),
            VMEM(rows, jnp.float32),
            pltpu.SemaphoreType.DMA((SUBSTEPS, 4)),
            pltpu.SemaphoreType.DMA((SUBSTEPS, 4)),
        ],
        compiler_params=pltpu.CompilerParams(
            collective_id=collective_id, has_side_effects=True
        ),
        name="substeps",
    )(displacement, velocity, stiff, loading)


def normal_speeds(velocity, wet_normal, node):
    parts, breadth, height, width = velocity.shape
    flattened = velocity[..., -LOADS:].reshape(parts, breadth * height, LOADS)
    picked = jnp.take(flattened, node, axis=1)
    speeds = (
        wet_normal[0][:, None] * picked[0]
        + wet_normal[1][:, None] * picked[1]
        + wet_normal[2][:, None] * picked[2]
    )
    return speeds.T


def node_loads(pressure, wet_normal, node, breadth, height):
    count = height * breadth
    one_hot = (
        lax.broadcasted_iota(jnp.int32, (count, node.shape[0]), 0) == node[None, :]
    ).astype(jnp.float32)
    contribution = -(wet_normal[:, None, :] * pressure[None, :, :])
    loading = jnp.einsum("pw,kqw->kpq", one_hot, contribution, precision=lax.Precision.HIGHEST)
    loading = loading.reshape(3, breadth, height, LOADS)
    return jnp.pad(loading, ((0, 0), (0, 0), (0, 0), (LOADS, 0)))


def on_device(shape, displacement, velocity, stiffness, wet_position, wet_normal, wet_area, wet_map):
    height, breadth = displacement.shape[1:3]
    displacement = displacement.transpose(0, 2, 1, 3)
    velocity = velocity.transpose(0, 2, 1, 3)
    stiff = jnp.broadcast_to(stiffness.T[:, :, None], (breadth, height, 2 * LOADS))
    node = (wet_map % breadth) * height + wet_map // breadth
    scaled = wet_normal * (wet_area * (1.0 / SPHERE_AREA))[None, :]
    geometry = jnp.concatenate(
        [wet_position, scaled, jnp.zeros((2, wet_position.shape[1]), jnp.float32)], axis=0
    )
    tiles = None
    for repeat in range(COUPLED):
        speeds = normal_speeds(velocity, wet_normal, node)
        rounded = speeds.astype(jnp.bfloat16)
        if repeat == 0:
            gathered, sources, targets = gather(shape, geometry, rounded, 0)
            sources = sources.transpose(0, 2, 1).reshape(-1, geometry.shape[0])
            tiles, partial_value = tile_and_product(sources, targets, gathered)
        else:
            (gathered,) = gather(shape, None, rounded, 1)
            partial_value = product(tiles, gathered)
        received = reduce_scatter(shape, partial_value, 2)
        pressure = 0.5 * speeds + received
        loading = node_loads(pressure, wet_normal, node, breadth, height)
        displacement, velocity = substeps(shape, displacement, velocity, stiff, loading, 3)
    return (displacement.transpose(0, 2, 1, 3), velocity.transpose(0, 2, 1, 3))


def solution(mesh):
    sizes = mesh.shape
    shape = (sizes["tcol"], sizes["group"] * sizes["trow"], sizes["trow"])
    state = P(None, ("group", "trow"), "tcol", None)
    wet = ("group", "trow", "tcol")
    return jax.shard_map(
        functools.partial(on_device, shape),
        mesh=mesh,
        in_specs=(
            state,
            state,
            P(("group", "trow"), "tcol"),
            P(None, wet),
            P(None, wet),
            P(wet),
            P(wet),
        ),
        out_specs=(state, state),
        check_vma=False,
    )
```

time: 491 us -> 170 us (0.35)
  waiting for transfers between devices: 150 us -> 0 us
  blocking collectives: 148 us -> 0 us
  Pallas kernels: 0 us -> 143 us
  starting transfers between devices: 97.2 us -> 0 us
  other arithmetic: 33 us -> 6.42 us
  matrix products: 19.5 us -> 0.65 us
  between operations: 15.3 us -> 0.8 us
    all_gather x6 -> x0, blocking collectives: 148 us -> none  [the longest x2 60.8 us: on_device(): gathered = lax.all_gather(speed_rounded, 'tcol', axis=1, tiled=True)]
    pallas_call x0 -> x8, Pallas kernels: none -> 143 us  [the longest x2 76.8 us: substeps(): pl.pallas_call(functools.partial(substeps_kernel, shape), out_shape=(stat...]
    ppermute x32 -> x0, waiting for transfers between devices: 142 us -> none  [the longest x16 118 us: padded_2(): after = lax.ppermute(first, axis, down)]
    ppermute x32 -> x0, starting transfers between devices: 97.1 us -> none  [the longest x16 60.9 us: padded_2(): after = lax.ppermute(first, axis, down)]
    dot_general x4 -> x0, matrix products: 18.8 us -> none  [accumulate(): partial_value = jnp.dot(gathered, tile, preferred_element_type=jnp.float32)]
    sub x8 -> x0, other arithmetic: 18 us -> none  [advance(): -(stiffness_grid * in_plane)]
    slice x45 -> x2, local copies, waits for them, and re-layouts: 14.5 us -> 1.33 us  [normal_speeds(): flattened = velocity[..., -LOADS:].reshape(parts, breadth * height, LOADS)]
    reduce_scatter x2 -> x0, waiting for transfers between devices: 7.89 us -> none  [on_device(): lax.psum_scatter(partial_value, ('group', 'trow'), scatter_dimension=1, t...]
  transfers between devices with their start and end apart: 34 -> 0, of which waited for: 23 -> 0; matrix products, arithmetic and copies ran while one was open for 10% -> 0% of each run, Pallas kernels for 0% -> 0%
where the time goes in v1:
time: 170 us; the launch traced here: 169 us
  Pallas kernels  143 us (84%)
  local copies, waits for them, and re-layouts  18.5 us (11%)
  other arithmetic  6.42 us (4%)
    pallas_call x2, Pallas kernels, substeps(): pl.pallas_call(functools.partial(substeps_kernel, shape), out_shape=(stat...  76.8 us
    pallas_call x1, Pallas kernels, tile_and_product(): pl.pallas_call(tile_kernel, grid=(row_count,), out_shape=(jax.ShapeDtypeS...  24 us
    pallas_call x2, Pallas kernels, gather(): pl.pallas_call(functools.partial(gather_kernel, shape, with_geometry), ou...  21.3 us
    pallas_call x2, Pallas kernels, reduce_scatter(): pl.pallas_call(functools.partial(reduce_kernel, shape), out_shape=jax.Sha...  13.7 us
    pallas_call x1, Pallas kernels, product(): pl.pallas_call(product_kernel, grid=(row_count,), out_shape=jax.ShapeDtyp...  6.93 us
    unnamed x6, local copies, waits for them, and re-layouts  4.95 us

profile of v1, /device:TPU:20, one launch (start us, length us, event | category | flops | bytes accessed | tf_op | source)
XLA Modules:
  0.0 169.2 jit_solution(1971556009809041094)
XLA Ops:
  1.4 0.7 compare_and_fusion
  2.1 0.7 broadcast_multiply_fusion
  2.8 0.8 fusion.28
  3.6 1.4 maximum_maximum_fusion.refs_0_
  5.0 1.4 broadcast_in_dim.13.stiff_ref
  6.4 2.7 %copy_bitcast_fusion = (f32[3,8,32,256]{3,2,1,0:T(8,128)S(1)}, f32[3,8,32,256]{3,2,1,0:T(8,128)}) fusion(f32[3,32,8,256]{3,2,1,0:T(8,128)} %param.10, f32[3,32,8,256]{3,2,1,0:T(8,128)} %param.9), kind=kLoop, calls=%fused_computation.4 | loop fusion | bytes 3145728 | tf_op jit(solution)/shard_map/transpose | solution.py:515
  9.6 1.0 gather_fusion
  11.4 11.5 %gather_geometry.1 = (bf16[8,64,256]{2,1,0:T(8,128)(2,1)}, f32[8,8,256]{2,1,0:T(8,128)}, f32[4,8,256]{2,1,0:T(8,128)}) custom-call(f32[8,256]{1,0:T(8,128)} %maximum_maximum_fusion.refs_0_, bf16[64,256]{1,0:T(8,128)(2,1)} %get-tuple-element.27.refs_1_), custom_call_target="tpu_custom_call" | custom-call | tf_op jit(solution)/shard_map/gather_geometry/pallas_call | solution.py:123
  22.9 2.1 %copy.20 = f32[8,256,8]{2,1,0:T(8,128)} copy(f32[8,256,8]{1,2,0:T(8,128)} %bitcast.89) | data formatting | bytes 131072 | tf_op jit(solution)/shard_map/transpose | solution.py:528
  25.1 24.0 %tile_and_product.1 = (bf16[4,2048,256]{2,1,0:T(8,128)(2,1)}, f32[4,64,256]{2,1,0:T(8,128)}) custom-call(f32[2048,8]{1,0:T(8,128)} %bitcast.82, f32[4,8,256]{2,1,0:T(8,128)} %get-tuple-element.13.target_ref, bf16[8,64,256]{2,1,0:T(8,128)(2,1)} %get-tuple-element.14.speeds_ref), custom_call_target="tpu_custom_call" | custom-call | tf_op jit(solution)/shard_map/tile_and_product/pallas_call | solution.py:195
  49.1 6.9 %reduce_scatter.2 = f32[64,256]{1,0:T(8,128)} custom-call(f32[4,64,256]{2,1,0:T(8,128)} %get-tuple-element.15.partial_ref), custom_call_target="tpu_custom_call" | custom-call | tf_op jit(solution)/shard_map/reduce_scatter/pallas_call | solution.py:261
  56.0 0.9 bitcast_add_fusion.1
  57.3 0.9 pad.7.load_ref
  58.3 39.1 %substeps.2 = (f32[3,8,32,256]{3,2,1,0:T(8,128)}, f32[3,8,32,256]{3,2,1,0:T(8,128)}) custom-call(f32[3,8,32,256]{3,2,1,0:T(8,128)} %get-tuple-element.35.u_in, f32[3,8,32,256]{3,2,1,0:T(8,128)} %copy-done, f32[8,32,128]{2,1,0:T(8,128)} %broadcast_in_dim.13.stiff_ref, f32[3,8,32,128]{3,2,1,0:T(8,128)} %pad.7.load_ref), custom_call_target="tpu_custom_call" | custom-call | tf_op jit(solution)/shard_map/substeps/pallas_call | solution.py:467
  97.3 1.2 slice.43
  98.8 1.0 gather_fusion.1
  100.6 9.8 %gather_speeds.1.speeds_ref = bf16[8,64,256]{2,1,0:T(8,128)(2,1)} custom-call(bf16[64,256]{1,0:T(8,128)(2,1)} %get-tuple-element.25.refs_0_), custom_call_target="tpu_custom_call" | custom-call | tf_op jit(solution)/shard_map/gather_speeds/pallas_call | solution.py:123
  110.4 6.9 %product.1.partial_ref = f32[4,64,256]{2,1,0:T(8,128)} custom-call(bf16[8,64,256]{2,1,0:T(8,128)(2,1)} %gather_speeds.1.speeds_ref, bf16[4,2048,256]{2,1,0:T(8,128)(2,1)} %get-tuple-element.18.tile_ref), custom_call_target="tpu_custom_call" | custom-call | tf_op jit(solution)/shard_map/product/pallas_call | solution.py:211
  117.3 6.9 %reduce_scatter.3 = f32[64,256]{1,0:T(8,128)} custom-call(f32[4,64,256]{2,1,0:T(8,128)} %product.1.partial_ref), custom_call_target="tpu_custom_call" | custom-call | tf_op jit(solution)/shard_map/reduce_scatter/pallas_call | solution.py:261
  124.2 0.9 bitcast_add_fusion
  125.6 0.9 pad.8.load_ref
  126.5 37.7 %substeps.3 = (f32[3,8,32,256]{3,2,1,0:T(8,128)}, f32[3,8,32,256]{3,2,1,0:T(8,128)}) custom-call(f32[3,8,32,256]{3,2,1,0:T(8,128)} %get-tuple-element.16.u_in, f32[3,8,32,256]{3,2,1,0:T(8,128)} %get-tuple-element.17.v_in, f32[8,32,128]{2,1,0:T(8,128)} %broadcast_in_dim.13.stiff_ref, f32[3,8,32,128]{3,2,1,0:T(8,128)} %pad.8.load_ref), custom_call_target="tpu_custom_call" | custom-call | tf_op jit(solution)/shard_map/substeps/pallas_call | solution.py:467
  164.2 2.5 %copy.25 = f32[3,32,8,256]{3,2,1,0:T(8,128)} copy(f32[3,32,8,256]{3,1,2,0:T(8,128)} %bitcast.88) | data formatting | bytes 1572864
  166.7 2.5 %copy.26 = f32[3,32,8,256]{3,2,1,0:T(8,128)} copy(f32[3,32,8,256]{3,1,2,0:T(8,128)} %bitcast.87) | data formatting | bytes 1572864
  (22 shorter events, 4.1 us)
Async XLA Ops:
  9.1 49.1 %copy-start = (f32[3,8,32,256]{3,2,1,0:T(8,128)}, f32[3,8,32,256]{3,2,1,0:T(8,128)S(1)}, u32[]{:S(2)}) copy-start(f32[3,8,32,256]{3,2,1,0:T(8,128)S(1)} %get-tuple-element.34.v_in) | copy-start | bytes 2359300
  9.1 47.7 %copy-start.1 = (f32[3,256]{1,0:T(4,128)S(1)}, f32[3,256]{1,0:T(4,128)}, u32[]{:S(2)}) copy-start(f32[3,256]{1,0:T(4,128)} %param.13) | copy-start | bytes 9220

commit v2 on v0

v2 whole, which is shorter than its diff:
```python
import functools
import math

import jax
import jax.numpy as jnp
from jax import lax
from jax.experimental import pallas as pl
from jax.experimental.pallas import tpu as pltpu
from jax.sharding import PartitionSpec as P

LOADS = 64
SUBSTEPS = 4
COUPLED = 2

SPHERE_AREA = 4.0 * math.pi
SMOOTHING = 0.1
TIME_STEP = 0.3
THICKNESS = 0.5
SPLINE_TAPS = (2.0 / 3.0, -1.0 / 12.0, -1.0 / 12.0, -1.0 / 6.0)
REACH = 3
PAD = 8
MESH = pl.DeviceIdType.MESH
VMEM = pltpu.VMEM


def row_device(index, trow_count):
    return {"group": index // trow_count, "trow": lax.rem(index, trow_count)}


def whole_spec():
    return pl.BlockSpec(memory_space=pltpu.VMEM)


HIGHEST = lax.Precision.HIGHEST


def coupled_kernel(
    shape, u_in, v_in, stiff_ref, position_ref, normal_ref, area_ref, node_ref, u_out, v_out,
    field, speed_now, work, load, col_out, col_in, row_out, row_in,
    geometry, sources, targets, target_cols, normal_cols, pick, spread,
    own_speeds, packed_out, packed_in, unpacked, tiles, partial_out, partial_in,
    halo_send, halo_recv, geo_send, geo_recv, speed_send, speed_recv, part_send, part_recv
):
    col_count, row_count, trow_count = shape
    parts, breadth, height, width = speed_now.shape
    half = width // 2
    points = geometry.shape[1]
    count = breadth * height
    col = lax.axis_index("tcol")
    row = lax.axis_index("group") * trow_count + lax.axis_index("trow")
    present = (col > 0, col < col_count - 1, row > 0, row < row_count - 1)
    peers = (
        {"tcol": jnp.maximum(col - 1, 0)},
        {"tcol": jnp.minimum(col + 1, col_count - 1)},
        row_device(jnp.maximum(row - 1, 0), trow_count),
        row_device(jnp.minimum(row + 1, row_count - 1), trow_count),
    )
    middle = pl.ds(PAD, height)

    def col_peer(d):
        return {"tcol": lax.rem(col + d, col_count)}

    def row_peer(d):
        return row_device(lax.rem(row + d, row_count), trow_count)

    barrier = pltpu.get_barrier_semaphore()

    @pl.loop(1, col_count)
    def _(d):
        pl.semaphore_signal(barrier, inc=1, device_id=col_peer(d), device_id_type=MESH)

    @pl.loop(1, row_count)
    def _(d):
        pl.semaphore_signal(barrier, inc=1, device_id=row_peer(d), device_id_type=MESH)

    geometry[0:3, :] = position_ref[...]
    geometry[3:6, :] = normal_ref[...] * (area_ref[...] * (1.0 / SPHERE_AREA))
    geometry[6:8, :] = jnp.zeros((2, points), jnp.float32)
    pl.semaphore_wait(barrier, col_count + row_count - 2)

    def geo_copy(kind, d):
        return pltpu.make_async_remote_copy(
            src_ref=geometry,
            dst_ref=sources.at[col] if kind == 0 else targets.at[row],
            send_sem=geo_send.at[kind, d],
            recv_sem=geo_recv.at[kind, d],
            device_id=col_peer(d) if kind == 0 else row_peer(d),
            device_id_type=MESH,
        )

    def speed_copy(repeat, d):
        return pltpu.make_async_remote_copy(
            src_ref=packed_out.at[repeat],
            dst_ref=packed_in.at[repeat, col],
            send_sem=speed_send.at[repeat, d],
            recv_sem=speed_recv.at[repeat, d],
            device_id=col_peer(d),
            device_id_type=MESH,
        )

    def part_copy(repeat, d):
        return pltpu.make_async_remote_copy(
            src_ref=partial_out.at[repeat, lax.rem(row + d, row_count)],
            dst_ref=partial_in.at[repeat, d],
            send_sem=part_send.at[repeat, d],
            recv_sem=part_recv.at[repeat, d],
            device_id=row_peer(d),
            device_id_type=MESH,
        )

    for kind, total in ((1, row_count), (0, col_count)):

        @pl.loop(1, total)
        def _(d):
            geo_copy(kind, d).start()

    sources[col] = geometry[...]
    targets[row] = geometry[...]

    field[...] = jnp.zeros_like(field)
    for part in range(parts):
        for j in range(breadth):
            for lanes in range(2):
                lines = pl.ds(lanes * breadth + j, height, stride=2 * breadth)
                cut = pl.ds(lanes * half, half)
                field[part, REACH + j, middle, cut] = u_in[part, lines, :]
                speed_now[part, j, :, cut] = v_in[part, lines, :]
    for side in range(2):

        @pl.when(jnp.logical_not(present[side]))
        def _():
            col_in[:, side] = jnp.zeros((col_in.shape[0],) + col_in.shape[2:], col_in.dtype)

    def as_column(line):
        return jnp.broadcast_to(line, (half, line.shape[1])).T

    for part in range(parts):
        normal_cols[part] = as_column(normal_ref[part : part + 1, :])
    spread[...] = (
        lax.broadcasted_iota(jnp.int32, (count, points), 0) == node_ref[...]
    ).astype(jnp.float32)
    pick[...] = spread[...].T

    def copy(step, side):
        out_buffer, in_buffer = (col_out, col_in) if side < 2 else (row_out, row_in)
        own, other = side % 2, 1 - side % 2
        return pltpu.make_async_remote_copy(
            src_ref=out_buffer.at[step, own],
            dst_ref=in_buffer.at[step, other],
            send_sem=halo_send.at[step, side],
            recv_sem=halo_recv.at[step, (side // 2) * 2 + other],
            device_id=peers[side],
            device_id_type=MESH,
        )

    def arrival(step, side):
        out_buffer, in_buffer = (col_out, col_in) if side < 2 else (row_out, row_in)
        return pltpu.make_async_remote_copy(
            src_ref=out_buffer.at[step, side % 2],
            dst_ref=in_buffer.at[step, side % 2],
            send_sem=halo_send.at[step, side],
            recv_sem=halo_recv.at[step, side],
            device_id=peers[side],
            device_id_type=MESH,
        )

    lane = lax.broadcasted_iota(jnp.int32, (height, half), 1)
    low = lane < half // 2
    low_half = lax.broadcasted_iota(jnp.int32, (points // 2, half), 1) < half // 2

    def pack(value):
        turned = pltpu.roll(value[points // 2 :], half // 2, 1)
        return jnp.where(low_half, turned, value[: points // 2])

    def tile(r):
        group = 32

        def block(index, carry):
            source = index // (points // half)
            lanes = pl.ds(pl.multiple_of(lax.rem(index, points // half) * half, half), half)
            line = [sources[source, k : k + 1, lanes] for k in range(6)]

            def rows_of(g, inner):
                rows = pl.ds(pl.multiple_of(g * group, group), group)
                dx = target_cols[r, 0, rows, :] - line[0]
                dy = target_cols[r, 1, rows, :] - line[1]
                dz = target_cols[r, 2, rows, :] - line[2]
                numerator = line[3] * dx + line[4] * dy + line[5] * dz
                squared = dx * dx + dy * dy + dz * dz + SMOOTHING * SMOOTHING
                inverse = lax.rsqrt(squared)
                value = numerator * inverse * (inverse * inverse)
                tiles[r, source, rows, lanes] = value.astype(jnp.bfloat16)
                return inner

            return lax.fori_loop(0, points // group, rows_of, carry, unroll=2)

        lax.fori_loop(0, col_count * (points // half), block, 0)

    def substep(step):
        for side, first in ((0, REACH), (1, breadth)):

            @pl.when(present[side])
            def _():
                for part in range(parts):
                    for j in range(REACH):
                        col_out[step, side, part, j] = field[part, first + j, middle, :].astype(
                            col_out.dtype
                        )
                copy(step, side).start()

        for side, first in ((2, PAD), (3, PAD + height - REACH)):

            @pl.when(present[side])
            def _():
                for part in range(parts):
                    for j in range(breadth):
                        row_out[
                            step, side - 2, part, j // 2, (j % 2) * 4 : (j % 2) * 4 + REACH, :
                        ] = field[part, REACH + j, first : first + REACH, :]
                copy(step, side).start()

        def local(index, carry):
            part = index // breadth
            column = lax.rem(index, breadth)
            a = field[part, REACH + column, middle, 0:half]
            b = field[part, REACH + column, middle, half:width]
            turned_a = pltpu.roll(a, half // 2, 1)
            turned_b = pltpu.roll(b, half // 2, 1)
            between = jnp.where(low, turned_a, turned_b)
            edge_a = jnp.where(low, a, turned_a)
            edge_b = jnp.where(low, turned_b, b)
            stiff = stiff_ref[column]
            for lanes, here, edge in ((0, a, edge_a), (1, b, edge_b)):
                cut = pl.ds(lanes * half, half)
                summed = (2.0 * SPLINE_TAPS[0]) * here
                for offset in range(1, REACH + 1):
                    summed = summed + SPLINE_TAPS[offset] * (
                        field[part, REACH + column + offset, middle, cut]
                        + field[part, REACH + column - offset, middle, cut]
                    )
                value = -(stiff * summed) - THICKNESS * (2.0 * here - between - edge)
                if lanes == 1:
                    value = value + load[part, column]
                work[part, column, :, cut] = speed_now[part, column, :, cut] + TIME_STEP * value
            return carry

        lax.fori_loop(0, parts * breadth, local, 0)

        for side, first in ((2, PAD - REACH), (3, PAD + height)):

            @pl.when(present[side])
            def _():
                arrival(step, side).wait_recv()
                for part in range(parts):
                    for j in range(breadth):
                        field[part, REACH + j, first : first + REACH, :] = row_in[
                            step, side - 2, part, j // 2, (j % 2) * 4 : (j % 2) * 4 + REACH, :
                        ]

        def along_rows(index, carry):
            part = index // breadth
            column = lax.rem(index, breadth)
            stiff = stiff_ref[column] * (-TIME_STEP)
            for lanes in range(2):
                cut = pl.ds(lanes * half, half)
                summed = 0.0
                for offset in range(1, REACH + 1):
                    summed = summed + SPLINE_TAPS[offset] * (
                        field[part, REACH + column, pl.ds(PAD + offset, height), cut]
                        + field[part, REACH + column, pl.ds(PAD - offset, height), cut]
                    )
                work[part, column, :, cut] += stiff * summed
            return carry

        lax.fori_loop(0, parts * breadth, along_rows, 0)

        for side in range(2):

            @pl.when(present[side])
            def _():
                arrival(step, side).wait_recv()

        def finish(part, carry):
            for column in range(breadth):
                stiff = stiff_ref[column] * (-TIME_STEP)
                for lanes in range(2):
                    cut = pl.ds(lanes * half, half)
                    value = work[part, column, :, cut]
                    summed = None
                    for offset in range(1, REACH + 1):
                        for side, j in ((0, column - offset + REACH), (1, column + offset - breadth)):
                            inside = (column - offset < 0) if side == 0 else (column + offset >= breadth)
                            if inside:
                                term = SPLINE_TAPS[offset] * col_in[
                                    step, side, part, j, :, cut
                                ].astype(jnp.float32)
                                summed = term if summed is None else summed + term
                    if summed is not None:
                        value = value + stiff * summed
                    speed_now[part, column, :, cut] = value
                    field[part, REACH + column, middle, cut] += TIME_STEP * value
            return carry

        lax.fori_loop(0, parts, finish, 0)

    for repeat in range(COUPLED):
        speeds = jnp.zeros((points, half), jnp.float32)
        for part in range(parts):
            outer = speed_now[part, :, :, half:width].reshape(count, half)
            picked = jnp.dot(
                pick[...], outer, precision=HIGHEST, preferred_element_type=jnp.float32
            )
            speeds = speeds + normal_cols[part] * picked
        own_speeds[...] = speeds
        packed_out[repeat] = pack(speeds).astype(packed_out.dtype)

        @pl.loop(1, col_count)
        def _(d):
            speed_copy(repeat, d).start()

        packed_in[repeat, col] = packed_out[repeat]

        if repeat == 0:

            @pl.loop(1, row_count)
            def _(d):
                geo_copy(1, d).wait_recv()

            @pl.loop(1, col_count)
            def _(d):
                geo_copy(0, d).wait_recv()

            @pl.loop(0, row_count)
            def _(r):
                for k in range(3):
                    target_cols[r, k] = as_column(targets[r, k : k + 1, :])

            tile(lax.rem(row + 1, row_count))

        @pl.loop(1, col_count)
        def _(d):
            speed_copy(repeat, d).wait_recv()

        @pl.loop(0, col_count)
        def _(c):
            value = packed_in[repeat, c].astype(jnp.float32)
            unpacked[c, 0 : points // 2, :] = value.astype(jnp.bfloat16)
            unpacked[c, points // 2 : points, :] = pltpu.roll(value, half // 2, 1).astype(
                jnp.bfloat16
            )

        @pl.loop(1, row_count + 1)
        def _(d):
            r = lax.rem(row + d, row_count)
            total = jnp.zeros((points, half), jnp.float32)
            for c in range(col_count):
                total = total + jnp.dot(
                    tiles[r, c], unpacked[c], preferred_element_type=jnp.float32
                )
            partial_out[repeat, r] = pack(total)

            @pl.when(d < row_count)
            def _():
                part_copy(repeat, d).start()
                if repeat == 0:
                    tile(lax.rem(r + 1, row_count))

        received = partial_out[repeat, row]
        for d in range(1, row_count):
            part_copy(repeat, d).wait_recv()
            received = received + partial_in[repeat, d]
        low_points = jnp.concatenate([low_half, low_half], axis=0)
        both = jnp.concatenate([received, pltpu.roll(received, half // 2, 1)], axis=0)
        pressure = jnp.where(low_points, 0.0, 0.5 * own_speeds[...] + both)
        for part in range(parts):
            loading = jnp.dot(
                spread[...], -(normal_cols[part] * pressure),
                precision=HIGHEST, preferred_element_type=jnp.float32,
            )
            load[part] = loading.reshape(breadth, height, half)

        @pl.loop(repeat * SUBSTEPS, (repeat + 1) * SUBSTEPS)
        def _(step):
            substep(step)

    for part in range(parts):
        for j in range(breadth):
            for lanes in range(2):
                lines = pl.ds(lanes * breadth + j, height, stride=2 * breadth)
                cut = pl.ds(lanes * half, half)
                u_out[part, lines, :] = field[part, REACH + j, middle, cut]
                v_out[part, lines, :] = speed_now[part, j, :, cut]

    @pl.loop(0, COUPLED * SUBSTEPS)
    def _(step):
        for side in range(4):

            @pl.when(present[side])
            def _():
                copy(step, side).wait_send()

    @pl.loop(1, col_count)
    def _(d):
        geo_copy(0, d).wait_send()
        for repeat in range(COUPLED):
            speed_copy(repeat, d).wait_send()

    @pl.loop(1, row_count)
    def _(d):
        geo_copy(1, d).wait_send()
        for repeat in range(COUPLED):
            part_copy(repeat, d).wait_send()


def on_device(shape, displacement, velocity, stiffness, wet_position, wet_normal, wet_area, wet_map):
    col_count, row_count, _ = shape
    parts, height, breadth, width = displacement.shape
    half = width // 2
    points = wet_map.shape[0]
    steps = COUPLED * SUBSTEPS
    stiff = jnp.broadcast_to(stiffness.T[:, :, None], (breadth, height, half))
    node = (wet_map % breadth) * height + wet_map // breadth

    def split(state):
        tiled = state.reshape(parts, height, breadth, 2, half).transpose(0, 1, 3, 2, 4)
        return tiled.reshape(parts, height * 2 * breadth, half)

    def joined(state):
        tiled = state.reshape(parts, height, 2, breadth, half).transpose(0, 1, 3, 2, 4)
        return tiled.reshape(parts, height, breadth, width)

    state = jax.ShapeDtypeStruct((parts, height * 2 * breadth, half), jnp.float32)
    cols = (steps, 2, parts, REACH, height, width)
    rows = (steps, 2, parts, breadth // 2, 8, width)
    f32, bf16 = jnp.float32, jnp.bfloat16
    dma = pltpu.SemaphoreType.DMA
    u_new, v_new = pl.pallas_call(
        functools.partial(coupled_kernel, shape),
        out_shape=(state, state),
        in_specs=[whole_spec()] * 7,
        out_specs=(whole_spec(), whole_spec()),
        scratch_shapes=[
            VMEM((parts, breadth + 2 * REACH, height + 2 * PAD, width), f32),
            VMEM((parts, breadth, height, width), f32),
            VMEM((parts, breadth, height, width), f32),
            VMEM((parts, breadth, height, half), f32),
            VMEM(cols, bf16),
            VMEM(cols, bf16),
            VMEM(rows, f32),
            VMEM(rows, f32),
            VMEM((8, points), f32),
            VMEM((col_count, 8, points), f32),
            VMEM((row_count, 8, points), f32),
            VMEM((row_count, 3, points, half), f32),
            VMEM((parts, points, half), f32),
            VMEM((points, height * breadth), f32),
            VMEM((height * breadth, points), f32),
            VMEM((points, half), f32),
            VMEM((COUPLED, points // 2, half), bf16),
            VMEM((COUPLED, col_count, points // 2, half), bf16),
            VMEM((col_count, points, half), bf16),
            VMEM((row_count, col_count, points, points), bf16),
            VMEM((COUPLED, row_count, points // 2, half), f32),
            VMEM((COUPLED, row_count, points // 2, half), f32),
            dma((steps, 4)),
            dma((steps, 4)),
            dma((2, max(col_count, row_count))),
            dma((2, max(col_count, row_count))),
            dma((COUPLED, col_count)),
            dma((COUPLED, col_count)),
            dma((COUPLED, row_count)),
            dma((COUPLED, row_count)),
        ],
        compiler_params=pltpu.CompilerParams(
            collective_id=0, has_side_effects=True, vmem_limit_bytes=67043328
        ),
        name="coupled_steps",
    )(
        split(displacement), split(velocity), stiff,
        wet_position, wet_normal, wet_area[None, :], node[None, :],
    )
    return (joined(u_new), joined(v_new))


def solution(mesh):
    sizes = mesh.shape
    shape = (sizes["tcol"], sizes["group"] * sizes["trow"], sizes["trow"])
    state = P(None, ("group", "trow"), "tcol", None)
    wet = ("group", "trow", "tcol")
    return jax.shard_map(
        functools.partial(on_device, shape),
        mesh=mesh,
        in_specs=(
            state,
            state,
            P(("group", "trow"), "tcol"),
            P(None, wet),
            P(None, wet),
            P(wet),
            P(wet),
        ),
        out_specs=(state, state),
        check_vma=False,
    )
```

time: 491 us -> 108 us (0.22); the launches traced: 486 us -> 108 us
  waiting for transfers between devices: 150 us -> 0 us
  blocking collectives: 148 us -> 0 us
  Pallas kernels: 0 us -> 102 us
  starting transfers between devices: 97.2 us -> 0 us
  other arithmetic: 33 us -> 0.57 us
  matrix products: 19.5 us -> 0 us
  local copies, waits for them, and re-layouts: 22.9 us -> 4.44 us
  between operations: 15.3 us -> 0.66 us
    all_gather x6 -> x0, blocking collectives: 148 us -> none  [the longest x2 60.8 us: on_device(): gathered = lax.all_gather(speed_rounded, 'tcol', axis=1, tiled=True)]
    ppermute x32 -> x0, waiting for transfers between devices: 142 us -> none  [the longest x16 118 us: padded_2(): after = lax.ppermute(first, axis, down)]
    pallas_call x0 -> x1, Pallas kernels: none -> 102 us  [on_device(): pl.pallas_call(functools.partial(coupled_kernel, shape), out_shape=(state...]
    ppermute x32 -> x0, starting transfers between devices: 97.1 us -> none  [the longest x16 60.9 us: padded_2(): after = lax.ppermute(first, axis, down)]
    dot_general x6 -> x0, matrix products: 19.5 us -> none  [the longest x4 18.8 us: accumulate(): partial_value = jnp.dot(gathered, tile, preferred_element_type=jnp.float32)]
    sub x8 -> x0, other arithmetic: 18 us -> none  [advance(): -(stiffness_grid * in_plane)]
    slice x46 -> x0, local copies, waits for them, and re-layouts: 15.3 us -> none  [the longest x16 4.02 us: padded_2(): first = lax.slice_in_dim(array, 0, width, axis=dim)]
    reduce_scatter x2 -> x0, waiting for transfers between devices: 7.89 us -> none  [on_device(): lax.psum_scatter(partial_value, ('group', 'trow'), scatter_dimension=1, t...]
  transfers between devices with their start and end apart: 34 -> 0, of which waited for: 23 -> 0; matrix products, arithmetic and copies ran while one was open for 10% -> 0% of each run, Pallas kernels for 0% -> 0%
where the time goes in v2:
time: 108 us
  Pallas kernels  102 us (94%)
  local copies, waits for them, and re-layouts  4.44 us (4%)
    pallas_call x1, Pallas kernels, on_device(): pl.pallas_call(functools.partial(coupled_kernel, shape), out_shape=(state...  102 us
    unnamed x8, local copies, waits for them, and re-layouts  3.69 us

profile of v2, /device:TPU:20, one launch (start us, length us, event | category | flops | bytes accessed | tf_op | source)
XLA Modules:
  0.0 108.1 jit_solution(4434349017119581049)
XLA Ops:
  0.6 0.0 copy-start.2
  0.6 0.0 copy-start.1
  0.6 0.7 copy-done.2
  1.3 0.6 fusion.1
  1.9 0.0 copy-done.1
  1.9 0.8 broadcast_in_dim.12.stiff_ref
  2.6 102.4 %coupled_steps.1 = (f32[3,512,128]{2,1,0:T(8,128)}, f32[3,512,128]{2,1,0:T(8,128)}) custom-call(f32[3,512,128]{2,1,0:T(8,128)} %bitcast.25, f32[3,512,128]{2,1,0:T(8,128)} %bitcast.26, f32[8,32,128]{2,1,0:T(8,128)} %broadcast_in_dim.12.stiff_ref, f32[3,256]{1,0:T(4,128)} %position_ref.1, f32[3,256]{1,0:T(4,128)} %normal_ref.1, f32[1,256]{1,0:T(1,128)} %bitcast.29, ...), custom_call_target="tpu_custom_call" | custom-call | tf_op jit(solution)/shard_map/coupled_steps/pallas_call | solution.py:437
  105.0 0.0 copy-start
  105.0 2.1 %copy.11 = f32[3,32,8,256]{3,2,1,0:T(8,128)} copy(f32[3,32,8,256]{3,2,1,0:T(8,128)} %bitcast.24) | data formatting | bytes 1572864
  107.2 0.0 copy-done
  107.2 0.9 copy.12
Async XLA Ops:
  0.6 0.7 copy-start.2
  0.6 1.2 %copy-start.1 = (f32[32,8]{0,1:T(8,128)S(1)}, f32[32,8]{0,1:T(8,128)}, u32[]{:S(2)}) copy-start(f32[32,8]{0,1:T(8,128)} %param.9) | copy-start | bytes 3076
  105.0 2.1 %copy-start = (f32[3,512,128]{2,1,0:T(8,128)S(1)}, f32[3,512,128]{2,1,0:T(8,128)}, u32[]{:S(2)}) copy-start(f32[3,512,128]{2,1,0:T(8,128)} %get-tuple-element.5) | copy-start | bytes 2359300

commit v3 on v2

--- a/solution.py
+++ b/solution.py
@@ -129,7 +129,7 @@
 
         @pl.when(jnp.logical_not(present[side]))
         def _():
-            col_in[:, side] = jnp.zeros((col_in.shape[0],) + col_in.shape[2:], col_in.dtype)
+            col_in[:, :, side] = jnp.zeros(col_in.shape[:2] + col_in.shape[3:], col_in.dtype)
 
     def as_column(line):
         return jnp.broadcast_to(line, (half, line.shape[1])).T
@@ -141,25 +141,15 @@
     ).astype(jnp.float32)
     pick[...] = spread[...].T
 
-    def copy(step, side):
+    def halo_copy(step, side, part, arriving):
         out_buffer, in_buffer = (col_out, col_in) if side < 2 else (row_out, row_in)
-        own, other = side % 2, 1 - side % 2
+        own = side % 2
+        other = own if arriving else 1 - own
         return pltpu.make_async_remote_copy(
-            src_ref=out_buffer.at[step, own],
-            dst_ref=in_buffer.at[step, other],
-            send_sem=halo_send.at[step, side],
-            recv_sem=halo_recv.at[step, (side // 2) * 2 + other],
-            device_id=peers[side],
-            device_id_type=MESH,
-        )
-
-    def arrival(step, side):
-        out_buffer, in_buffer = (col_out, col_in) if side < 2 else (row_out, row_in)
-        return pltpu.make_async_remote_copy(
-            src_ref=out_buffer.at[step, side % 2],
-            dst_ref=in_buffer.at[step, side % 2],
-            send_sem=halo_send.at[step, side],
-            recv_sem=halo_recv.at[step, side],
+            src_ref=out_buffer.at[step, part, own],
+            dst_ref=in_buffer.at[step, part, other],
+            send_sem=halo_send.at[step, part, side],
+            recv_sem=halo_recv.at[step, part, (side // 2) * 2 + other],
             device_id=peers[side],
             device_id_type=MESH,
         )
@@ -196,32 +186,29 @@
 
         lax.fori_loop(0, col_count * (points // half), block, 0)
 
-    def substep(step):
+    def send_halos(step, part):
         for side, first in ((0, REACH), (1, breadth)):
 
             @pl.when(present[side])
             def _():
-                for part in range(parts):
-                    for j in range(REACH):
-                        col_out[step, side, part, j] = field[part, first + j, middle, :].astype(
-                            col_out.dtype
-                        )
-                copy(step, side).start()
+                for j in range(REACH):
+                    col_out[step, part, side, j] = field[part, first + j, middle, :].astype(
+                        col_out.dtype
+                    )
+                halo_copy(step, side, part, False).start()
 
         for side, first in ((2, PAD), (3, PAD + height - REACH)):
 
             @pl.when(present[side])
             def _():
-                for part in range(parts):
-                    for j in range(breadth):
-                        row_out[
-                            step, side - 2, part, j // 2, (j % 2) * 4 : (j % 2) * 4 + REACH, :
-                        ] = field[part, REACH + j, first : first + REACH, :]
-                copy(step, side).start()
-
-        def local(index, carry):
-            part = index // breadth
-            column = lax.rem(index, breadth)
+                for j in range(breadth):
+                    row_out[
+                        step, part, side - 2, j // 2, (j % 2) * 4 : (j % 2) * 4 + REACH, :
+                    ] = field[part, REACH + j, first : first + REACH, :]
+                halo_copy(step, side, part, False).start()
+
+    def local(part):
+        def body(column, carry):
             a = field[part, REACH + column, middle, 0:half]
             b = field[part, REACH + column, middle, half:width]
             turned_a = pltpu.roll(a, half // 2, 1)
@@ -244,22 +231,20 @@
                 work[part, column, :, cut] = speed_now[part, column, :, cut] + TIME_STEP * value
             return carry
 
-        lax.fori_loop(0, parts * breadth, local, 0)
-
+        lax.fori_loop(0, breadth, body, 0)
+
+    def complete(step, part):
         for side, first in ((2, PAD - REACH), (3, PAD + height)):
 
             @pl.when(present[side])
             def _():
-                arrival(step, side).wait_recv()
-                for part in range(parts):
-                    for j in range(breadth):
-                        field[part, REACH + j, first : first + REACH, :] = row_in[
-                            step, side - 2, part, j // 2, (j % 2) * 4 : (j % 2) * 4 + REACH, :
-                        ]
-
-        def along_rows(index, carry):
-            part = index // breadth
-            column = lax.rem(index, breadth)
+                halo_copy(step, side, part, True).wait_recv()
+                for j in range(breadth):
+                    field[part, REACH + j, first : first + REACH, :] = row_in[
+                        step, part, side - 2, j // 2, (j % 2) * 4 : (j % 2) * 4 + REACH, :
+                    ]
+
+        def along_rows(column, carry):
             stiff = stiff_ref[column] * (-TIME_STEP)
             for lanes in range(2):
                 cut = pl.ds(lanes * half, half)
@@ -272,36 +257,32 @@
                 work[part, column, :, cut] += stiff * summed
             return carry
 
-        lax.fori_loop(0, parts * breadth, along_rows, 0)
+        lax.fori_loop(0, breadth, along_rows, 0)
 
         for side in range(2):
 
             @pl.when(present[side])
             def _():
-                arrival(step, side).wait_recv()
-
-        def finish(part, carry):
-            for column in range(breadth):
-                stiff = stiff_ref[column] * (-TIME_STEP)
-                for lanes in range(2):
-                    cut = pl.ds(lanes * half, half)
-                    value = work[part, column, :, cut]
-                    summed = None
-                    for offset in range(1, REACH + 1):
-                        for side, j in ((0, column - offset + REACH), (1, column + offset - breadth)):
-                            inside = (column - offset < 0) if side == 0 else (column + offset >= breadth)
-                            if inside:
-                                term = SPLINE_TAPS[offset] * col_in[
-                                    step, side, part, j, :, cut
-                                ].astype(jnp.float32)
-                                summed = term if summed is None else summed + term
-                    if summed is not None:
-                        value = value + stiff * summed
-                    speed_now[part, column, :, cut] = value
-                    field[part, REACH + column, middle, cut] += TIME_STEP * value
-            return carry
-
-        lax.fori_loop(0, parts, finish, 0)
+                halo_copy(step, side, part, True).wait_recv()
+
+        for column in range(breadth):
+            stiff = stiff_ref[column] * (-TIME_STEP)
+            for lanes in range(2):
+                cut = pl.ds(lanes * half, half)
+                value = work[part, column, :, cut]
+                summed = None
+                for offset in range(1, REACH + 1):
+                    for side, j in ((0, column - offset + REACH), (1, column + offset - breadth)):
+                        inside = (column - offset < 0) if side == 0 else (column + offset >= breadth)
+                        if inside:
+                            term = SPLINE_TAPS[offset] * col_in[
+                                step, part, side, j, :, cut
+                            ].astype(jnp.float32)
+                            summed = term if summed is None else summed + term
+                if summed is not None:
+                    value = value + stiff * summed
+                speed_now[part, column, :, cut] = value
+                field[part, REACH + column, middle, cut] += TIME_STEP * value
 
     for repeat in range(COUPLED):
         speeds = jnp.zeros((points, half), jnp.float32)
@@ -340,6 +321,10 @@
         @pl.loop(1, col_count)
         def _(d):
             speed_copy(repeat, d).wait_recv()
+
+        @pl.loop(0, parts)
+        def _(part):
+            send_halos(repeat * SUBSTEPS, part)
 
         @pl.loop(0, col_count)
         def _(c):
@@ -379,9 +364,20 @@
             )
             load[part] = loading.reshape(breadth, height, half)
 
-        @pl.loop(repeat * SUBSTEPS, (repeat + 1) * SUBSTEPS)
+            local(part)
+
+        last = (repeat + 1) * SUBSTEPS - 1
+
+        @pl.loop(repeat * SUBSTEPS, last + 1)
         def _(step):
-            substep(step)
+            @pl.loop(0, parts)
+            def _(part):
+                complete(step, part)
+
+                @pl.when(step < last)
+                def _():
+                    send_halos(step + 1, part)
+                    local(part)
 
     for part in range(parts):
         for j in range(breadth):
@@ -397,7 +393,8 @@
 
             @pl.when(present[side])
             def _():
-                copy(step, side).wait_send()
+                for part in range(parts):
+                    halo_copy(step, side, part, False).wait_send()
 
     @pl.loop(1, col_count)
     def _(d):
@@ -430,8 +427,8 @@
         return tiled.reshape(parts, height, breadth, width)
 
     state = jax.ShapeDtypeStruct((parts, height * 2 * breadth, half), jnp.float32)
-    cols = (steps, 2, parts, REACH, height, width)
-    rows = (steps, 2, parts, breadth // 2, 8, width)
+    cols = (steps, parts, 2, REACH, height, width)
+    rows = (steps, parts, 2, breadth // 2, 8, width)
     f32, bf16 = jnp.float32, jnp.bfloat16
     dma = pltpu.SemaphoreType.DMA
     u_new, v_new = pl.pallas_call(
@@ -462,8 +459,8 @@
             VMEM((row_count, col_count, points, points), bf16),
             VMEM((COUPLED, row_count, points // 2, half), f32),
             VMEM((COUPLED, row_count, points // 2, half), f32),
-            dma((steps, 4)),
-            dma((steps, 4)),
+            dma((steps, parts, 4)),
+            dma((steps, parts, 4)),
             dma((2, max(col_count, row_count))),
             dma((2, max(col_count, row_count))),
             dma((COUPLED, col_count)),

time: 108 us -> 100 us (0.926)
  Pallas kernels: 102 us -> 94 us
    pallas_call x1, Pallas kernels: 102 us -> 94 us  [on_device(): pl.pallas_call(functools.partial(coupled_kernel, shape), out_shape=(state...]
where the time goes in v3:
time: 100 us; the launch traced here: 99.7 us
  Pallas kernels  94 us (94%)
  local copies, waits for them, and re-layouts  4.44 us (4%)
    pallas_call x1, Pallas kernels, on_device(): pl.pallas_call(functools.partial(coupled_kernel, shape), out_shape=(state...  94 us
    unnamed x8, local copies, waits for them, and re-layouts  3.69 us

profile of v3, /device:TPU:20, one launch (start us, length us, event | category | flops | bytes accessed | tf_op | source)
XLA Modules:
  0.0 99.7 jit_solution(12988091751508363114)
XLA Ops:
  0.6 0.0 copy-start.2
  0.6 0.0 copy-start.1
  0.6 0.7 copy-done.2
  1.3 0.6 fusion.1
  1.9 0.0 copy-done.1
  1.9 0.8 broadcast_in_dim.12.stiff_ref
  2.6 94.0 %coupled_steps.1 = (f32[3,512,128]{2,1,0:T(8,128)}, f32[3,512,128]{2,1,0:T(8,128)}) custom-call(f32[3,512,128]{2,1,0:T(8,128)} %bitcast.25, f32[3,512,128]{2,1,0:T(8,128)} %bitcast.26, f32[8,32,128]{2,1,0:T(8,128)} %broadcast_in_dim.12.stiff_ref, f32[3,256]{1,0:T(4,128)} %position_ref.1, f32[3,256]{1,0:T(4,128)} %normal_ref.1, f32[1,256]{1,0:T(1,128)} %bitcast.29, ...), custom_call_target="tpu_custom_call" | custom-call | tf_op jit(solution)/shard_map/coupled_steps/pallas_call | solution.py:434
  96.7 0.0 copy-start
  96.7 2.1 %copy.11 = f32[3,32,8,256]{3,2,1,0:T(8,128)} copy(f32[3,32,8,256]{3,2,1,0:T(8,128)} %bitcast.24) | data formatting | bytes 1572864
  98.8 0.0 copy-done
  98.8 0.9 copy.12
Async XLA Ops:
  0.6 0.7 copy-start.2
  0.6 1.2 %copy-start.1 = (f32[32,8]{0,1:T(8,128)S(1)}, f32[32,8]{0,1:T(8,128)}, u32[]{:S(2)}) copy-start(f32[32,8]{0,1:T(8,128)} %param.9) | copy-start | bytes 3076
  96.7 2.1 %copy-start = (f32[3,512,128]{2,1,0:T(8,128)S(1)}, f32[3,512,128]{2,1,0:T(8,128)}, u32[]{:S(2)}) copy-start(f32[3,512,128]{2,1,0:T(8,128)} %get-tuple-element.5) | copy-start | bytes 2359300
